TPU v7x, 32 devices: a whole 2x2x4 slice. The times are simulated.
32 devices in a mesh: chan: 8 (over z, x), tm: 4 (over y, core).
Axes of the slice: x: 2, y: 2, z: 4, core: 2. Of those that a mesh axis runs over, the one named last changes fastest.
Arguments:
- raw_traces: bfloat16 [512, 16, 4096], P('chan', 'tm'), may hold values from -6 to 6
- owner_lists: int32 [8, 128], replicated, may hold values from -1 to 511, as said below
- source_owner: int32 [2], replicated, may hold values from 0 to 7
- source_slot: int32 [2, 8], replicated, may hold values from 0 to 31, as said below
Outputs:
- correlations: float32 [1024, 16, 256], P(('chan', 'tm'))
Inputs may be any that keep to these rules, and one draw needn't show every extreme that they name: `owner_lists`: row o lists the channels owned by owner o, live entries first and then -1; each of the 512 channels appears exactly once. A quarter of the rows hold 128 live entries, half of them 3 * 16 and a quarter 64 / 2. At most 16 live entries of one row lie in one block of 64 consecutive channels, and some row has exactly 16 in some block. `source_slot`: the 8 entries of a step are distinct and below 32, so they name live channels of that owner.
All inputs are finite; a program needn't handle non-finite values.
Results may differ from a plain program's by a relative error of at most 0.0046.
Values may be sent and summed in bfloat16 or wider, within the bound.
A program may use at most 64 MiB of HBM per device.

v0:
```python
import math

import jax
import jax.numpy as jnp
from jax import lax
from jax.sharding import PartitionSpec as P

L1 = 64
L2 = 64
L = 4096
HW = 64
LAGS = 256
STEPS = 2


EPSILON = 1e-06
TWO_PI = 2.0 * math.pi


def spread(value, axis, source):
    kept = jnp.where(lax.axis_index(axis) == source, value, 0).astype(value.dtype)
    return lax.psum(kept, axis)


def make_tables():
    sample = jnp.arange(L, dtype=jnp.int32)
    window_taper = 0.5 - 0.5 * jnp.cos(TWO_PI / L * (sample.astype(jnp.float32) + 0.5))
    inner_index = jnp.arange(L2, dtype=jnp.int32)
    first_angle = (
        TWO_PI / L2 * (inner_index[:, None] * inner_index[None, :] % L2).astype(jnp.float32)
    )
    first_table = jnp.concatenate([jnp.cos(first_angle), -jnp.sin(first_angle)], axis=1).astype(
        jnp.bfloat16
    )
    outer_index = jnp.arange(L1, dtype=jnp.int32)
    twist_angle = TWO_PI / L * (outer_index[:, None] * inner_index[None, :] % L).astype(jnp.float32)
    twist_cos = jnp.cos(twist_angle)
    twist_sin = jnp.sin(twist_angle)
    half_index = jnp.arange(L1 // 2, dtype=jnp.int32)
    second_angle = (
        TWO_PI / L1 * (outer_index[:, None] * half_index[None, :] % L1).astype(jnp.float32)
    )
    second_cos = jnp.cos(second_angle)
    second_sin = jnp.sin(second_angle)
    second_table = jnp.concatenate(
        [
            jnp.concatenate([second_cos, -second_sin], axis=1),
            jnp.concatenate([second_sin, second_cos], axis=1),
        ],
        axis=0,
    )
    span_bins = 2 * HW
    band_rows = jnp.arange(3 * span_bins, dtype=jnp.int32)
    band_cols = jnp.arange(span_bins, dtype=jnp.int32)
    band = (jnp.abs(band_rows[:, None] - span_bins - band_cols[None, :]) <= HW).astype(jnp.bfloat16)
    bin_index = jnp.arange(L // 2, dtype=jnp.int32)
    counts = (jnp.minimum(bin_index, HW) + jnp.minimum(L // 2 - 1 - bin_index, HW) + 1).astype(
        jnp.float32
    )
    lag_index = jnp.arange(LAGS, dtype=jnp.int32) - LAGS // 2
    lag_angle = TWO_PI / L * (bin_index[:, None] * lag_index[None, :] % L).astype(jnp.float32)
    weights = jnp.where(bin_index == 0, 1.0, 2.0).astype(jnp.float32)[:, None]
    inverse_table = jnp.concatenate(
        [weights * jnp.cos(lag_angle), -weights * jnp.sin(lag_angle)], axis=0
    )
    return (
        window_taper,
        first_table,
        twist_cos,
        twist_sin,
        second_table,
        band,
        counts,
        inverse_table,
    )


def whiten_block(row_block, tables):
    window_taper, first_table, twist_cos, twist_sin, second_table, band, counts = tables
    row_total = row_block.shape[0]
    half_bins = L // 2
    tapered = (
        (row_block.astype(jnp.float32) * window_taper)
        .astype(jnp.bfloat16)
        .reshape(row_total, L2, L1)
    )
    section_one = jnp.einsum(
        "nab,ak->nbk", tapered, first_table, preferred_element_type=jnp.float32
    )
    real_in = section_one[:, :, :L2]
    imag_in = section_one[:, :, L2:]
    turned = jnp.concatenate(
        [real_in * twist_cos + imag_in * twist_sin, imag_in * twist_cos - real_in * twist_sin],
        axis=1,
    )
    spectrum = jnp.einsum("ntk,tj->njk", turned, second_table, precision=lax.Precision.HIGHEST)
    real_part = spectrum[:, : L1 // 2].reshape(row_total, half_bins)
    imag_part = spectrum[:, L1 // 2 :].reshape(row_total, half_bins)
    magnitude = jnp.sqrt(real_part * real_part + imag_part * imag_part).astype(jnp.bfloat16)
    span_bins = 2 * HW
    blocks = magnitude.reshape(row_total, half_bins // span_bins, span_bins)
    padded = jnp.pad(blocks, ((0, 0), (1, 1), (0, 0)))
    joined = jnp.concatenate([padded[:, :-2], padded[:, 1:-1], padded[:, 2:]], axis=2)
    smooth = jnp.einsum("nbi,ij->nbj", joined, band, preferred_element_type=jnp.float32)
    smooth = smooth.reshape(row_total, half_bins) / counts
    denominator = smooth + EPSILON
    return jnp.concatenate([real_part / denominator, imag_part / denominator], axis=1).astype(
        jnp.bfloat16
    )


def whiten_rows(traces, tables):
    row_total = traces.shape[0]
    group_rows = math.gcd(row_total, 64)
    grouped = traces.reshape(row_total // group_rows, group_rows, traces.shape[1])
    whitened = lax.map(lambda row_block: whiten_block(row_block, tables), grouped)
    return whitened.reshape(row_total, traces.shape[1])


def correlate(own_rows, sources, inverse_table, norm_scale):
    count_rows = own_rows.shape[0]
    group_rows = math.gcd(count_rows, 8)
    half_bins = L // 2
    source_real = sources[:, :, :half_bins].astype(jnp.float32)
    source_imag = sources[:, :, half_bins:].astype(jnp.float32)

    def one_group(row_block):
        block_real = row_block[:, None, :, :half_bins].astype(jnp.float32)
        block_imag = row_block[:, None, :, half_bins:].astype(jnp.float32)
        cross_real = jnp.sum(
            block_real * source_real[None] + block_imag * source_imag[None], axis=2
        )
        cross_imag = jnp.sum(
            block_imag * source_real[None] - block_real * source_imag[None], axis=2
        )
        stacked = jnp.concatenate([cross_real, cross_imag], axis=2)
        return (
            jnp.einsum("nvk,kl->nvl", stacked, inverse_table, precision=lax.Precision.HIGHEST)
            * norm_scale
        )

    grouped = own_rows.reshape(
        count_rows // group_rows, group_rows, own_rows.shape[1], own_rows.shape[2]
    )
    result = lax.map(one_group, grouped)
    return result.reshape(count_rows, sources.shape[0], inverse_table.shape[1])


def send_plan(owner_lists, own_block, block_size, send_slots):
    source_block = jnp.floor_divide(owner_lists, block_size)
    matched = (owner_lists >= 0) & (source_block == own_block)
    ranking = jnp.cumsum(matched.astype(jnp.int32), axis=1) - 1
    offsets = owner_lists - own_block * block_size
    slot_ids = jnp.arange(send_slots, dtype=jnp.int32)
    chosen = matched[:, None, :] & (ranking[:, None, :] == slot_ids[None, :, None])
    send_rows = jnp.sum(jnp.where(chosen, offsets[:, None, :], 0), axis=2)
    send_live = jnp.any(chosen, axis=2)
    return (send_rows, send_live)


def receive_plan(owner_lists, own_block, block_size, send_slots):
    my_list = lax.dynamic_index_in_dim(owner_lists, own_block, 0, keepdims=False)
    living = my_list >= 0
    source_block = jnp.floor_divide(my_list, block_size)
    position = jnp.arange(my_list.shape[0], dtype=jnp.int32)
    earlier_same = (
        (source_block[:, None] == source_block[None, :])
        & (position[None, :] < position[:, None])
        & living[None, :]
    )
    earlier = jnp.sum(earlier_same.astype(jnp.int32), axis=1)
    receive_rows = jnp.where(living, source_block * send_slots + earlier, 0)
    return (receive_rows, living)


def pack_rows(values, send_rows, send_live):
    picked = jnp.take(values, send_rows.reshape(-1), axis=0)
    return jnp.where(send_live.reshape(-1)[:, None, None], picked, jnp.zeros((), values.dtype))


def place_rows(arrived, receive_rows, living):
    picked = jnp.take(arrived, receive_rows, axis=0)
    return jnp.where(living[:, None, None], picked, jnp.zeros((), arrived.dtype))


def body(raw_traces, owner_lists, source_owner, source_slot):
    block_size, window_count, length = raw_traces.shape
    owners = lax.axis_size("chan")
    time_shards = lax.axis_size("tm")
    capacity = owner_lists.shape[1]
    send_slots = (capacity + owners - 1) // owners
    own_block = lax.axis_index("chan")
    tables = make_tables()
    forward = tables[:7]
    inverse_table = tables[7]
    norm_scale = 1.0 / math.sqrt(window_count * time_shards * (length // 2))
    slot_share = capacity // time_shards
    send_rows, send_live = send_plan(owner_lists, own_block, block_size, send_slots)
    receive_rows, living = receive_plan(owner_lists, own_block, block_size, send_slots)
    outgoing = pack_rows(raw_traces, send_rows, send_live)
    arrived = lax.all_to_all(outgoing, "chan", split_axis=0, concat_axis=0, tiled=True)
    placed = place_rows(arrived, receive_rows, living)
    spectra = whiten_rows(placed.reshape(capacity * window_count, length), forward)
    spectra = spectra.reshape(capacity, window_count, length)
    pieces = []
    for step_index in range(STEPS):
        picked = jnp.take(spectra, source_slot[step_index], axis=0)
        sources = spread(picked, "chan", source_owner[step_index])

        def stack_term(first_row, row_count, sources=sources):
            return correlate(spectra, sources, inverse_table, norm_scale)

        pieces.append(
            lax.psum_scatter(
                stack_term(jnp.int32(0), slot_share * lax.axis_size("tm")),
                "tm",
                scatter_dimension=0,
                tiled=True,
            )
        )
    result = jnp.concatenate(pieces, axis=1)
    return result


def solution(mesh):
    return jax.shard_map(
        body,
        mesh=mesh,
        in_specs=(P("chan", "tm", None), P(), P(), P()),
        out_specs=P(("chan", "tm"), None, None),
        check_vma=False,
    )
```

profile of v0, /device:TPU:0, one launch (start us, length us, event | category | flops | bytes accessed | tf_op | source)
XLA Modules:
  0.0 585.9 jit_solution(15079302522156014081)
XLA Ops:
  9.1 7.5 %gather_fusion = bf16[128,4,4096]{2,1,0:T(4,128)(2,1)} fusion(bf16[64,4,4096]{2,1,0:T(4,128)(2,1)S(1)} %copy-done, s32[1024]{0:T(1024)S(1)} %pad_clamp_fusion.3), kind=kCustom, calls=%fused_computation.2 | custom fusion | bytes 8389120 | tf_op jit(solution)/shard_map/jit(_take)/gather | solution.py:177
  16.6 6.2 %select_select_fusion.1 = bf16[128,4,4096]{2,1,0:T(4,128)(2,1)} fusion(bf16[128,4,4096]{2,1,0:T(4,128)(2,1)} %gather_fusion, pred[128]{0:T(512)(128)(4,1)S(1)} %compare_and_fusion.4, pred[128]{0:T(512)(128)(4,1)S(1)} %broadcast_in_dim.142), kind=kLoop, calls=%fused_computation.94 | loop fusion | flops 4194304 | bytes 8388864 | tf_op jit(solution)/shard_map/jit(_where)/select_n | solution.py:178
  22.8 7.4 %all-to-all-start = ((bf16[128,4,4096]{2,1,0:T(4,128)(2,1)}), bf16[128,4,4096]{2,1,0:T(4,128)(2,1)}, u32[]{:S(2)}, u32[]{:S(2)}) async-start(bf16[128,4,4096]{2,1,0:T(4,128)(2,1)} %select_select_fusion.1), calls=%async_computation | async-start | bytes 8388608 | tf_op jit(solution)/shard_map/all_to_all | solution.py:201
  35.3 9.6 %cosine_multiply_fusion = (f32[2048,256]{1,0:T(8,128)}, f32[2048,256]{1,0:T(8,128)}) fusion(s32[256]{0:T(256)S(1)} %iota_add_fusion.1, f32[2048]{0:T(1024)S(1)} %get-tuple-element.347, f32[2048]{0:T(1024)S(1)} %get-tuple-element.348), kind=kLoop, calls=%fused_computation.102 | loop fusion | flops 8388608 | bytes 4211712 | tf_op jit(solution)/shard_map/mul | solution.py:64
  44.9 78.6 %all-to-all-done = bf16[128,4,4096]{2,1,0:T(4,128)(2,1)} async-done(((bf16[128,4,4096]{2,1,0:T(4,128)(2,1)}), bf16[128,4,4096]{2,1,0:T(4,128)(2,1)}, u32[]{:S(2)}, u32[]{:S(2)}) %all-to-all-start) | async-done | bytes 4194336 | tf_op jit(solution)/shard_map/all_to_all | solution.py:201
  123.5 9.8 %gather_fusion.1 = bf16[128,4,4096]{2,1,0:T(4,128)(2,1)} fusion(bf16[128,4,4096]{2,1,0:T(4,128)(2,1)} %all-to-all-done, s32[1024]{0:T(1024)S(1)} %pad_clamp_fusion.2), kind=kCustom, calls=%fused_computation.3 | custom fusion | bytes 8389120 | tf_op jit(solution)/shard_map/jit(_take)/gather | solution.py:182
  133.2 6.9 %gather.15 = bf16[8,64,4096]{2,1,0:T(8,128)(2,1)} reshape(bf16[128,4,4096]{2,1,0:T(4,128)(2,1)} %gather_fusion.1) | data formatting | bytes 8388608 | tf_op jit(solution)/shard_map/jit(_take)/gather | solution.py:182
  144.0 111.5 %while.39 = (s32[]{:T(128)}, bf16[8,64,4096]{2,1,0:T(8,128)(2,1)}, bf16[8,64,4096]{2,1,0:T(8,128)(2,1)}, bf16[64,128]{1,0:T(8,128)(2,1)S(1)}, f32[128,64]{0,1:T(8,128)S(1)}, /*index=5*/s32[384]{0:T(512)S(1)}) while((s32[]{:T(128)}, bf16[8,64,4096]{2,1,0:T(8,128)(2,1)}, bf16[8,64,4096]{2,1,0:T(8,128)(2,1)}, ...), condition=%wide.region_5.6_spmd.clone.clone.clone, body=%wide.region_4.5_spmd.clone.clone.sunk.clone | while | flops 578314240 | bytes 28805220 | solution.py:116
  255.5 7.2 %reshape_reshape.4 = bf16[128,4,4096]{2,1,0:T(4,128)(2,1)} reshape(bf16[8,64,4096]{2,1,0:T(8,128)(2,1)} %get-tuple-element.201) | data formatting | bytes 8388608 | tf_op jit(solution)/shard_map/reshape;reshape | solution.py:204
  274.4 7.3 %reshape_reshape_reshape.4 = bf16[16,8,4,4096]{3,2,1,0:T(4,128)(2,1)} reshape(bf16[8,64,4096]{2,1,0:T(8,128)(2,1)} %get-tuple-element.201) | data formatting | bytes 8388608 | tf_op jit(solution)/shard_map/reshape;reshape;reshape | solution.py:142
  281.8 60.8 %all-reduce.4.cloned.1.call-done = (bf16[8,4,4096]{2,1,0:T(4,128)(2,1)}, bf16[8,4,4096]{2,1,0:T(4,128)(2,1)}) async-done(((bf16[8,4,4096]{2,1,0:T(4,128)(2,1)}, bf16[8,4,4096]{2,1,0:T(4,128)(2,1)}), (bf16[8,4,4096]{2,1,0:T(4,128)(2,1)}, bf16[8,4,4096]{2,1,0:T(4,128)(2,1)})) %all-reduce.4.cloned.1.call-update) | async-done | bytes 524304 | tf_op jit(solution)/shard_map/psum | solution.py:22
  344.0 98.0 %while.37 = (s32[]{:T(128)}, f32[16,8,8,256]{3,2,1,0:T(8,128)S(1)}, bf16[16,8,4,4096]{3,2,1,0:T(4,128)(2,1)}, f32[8,4,2048]{2,0,1:T(8,128)S(1)}, f32[8,4,2048]{2,0,1:T(8,128)S(1)}, /*index=5*/f32[4096,256]{1,0:T(8,128)}) while((s32[]{:T(128)}, f32[16,8,8,256]{3,2,1,0:T(8,128)S(1)}, bf16[16,8,4,4096]{3,2,1,0:T(4,128)(2,1)}, ...), condition=%wide.region_10.12_spmd.clone, body=%wide.region_7.11_spmd.sunk.clone | while | flops 809648128 | bytes 8716365 | solution.py:145
  445.5 107.7 %while.38 = (s32[]{:T(128)}, f32[16,8,8,256]{3,2,1,0:T(8,128)}, bf16[16,8,4,4096]{3,2,1,0:T(4,128)(2,1)}, f32[8,4,2048]{2,0,1:T(8,128)S(1)}, f32[8,4,2048]{2,0,1:T(8,128)S(1)}, /*index=5*/f32[4096,256]{1,0:T(8,128)}) while((s32[]{:T(128)}, f32[16,8,8,256]{3,2,1,0:T(8,128)}, bf16[16,8,4,4096]{3,2,1,0:T(4,128)(2,1)}, ...), condition=%wide.region_16.18_spmd.clone, body=%wide.region_13.17_spmd.sunk.clone | while | flops 809648128 | bytes 8716873 | solution.py:145
  447.2 5.1 fusion.163
  460.7 5.1 fusion.163
  467.5 5.1 fusion.163
  474.2 5.1 fusion.163
  487.6 5.1 fusion.163
  514.6 5.1 fusion.163
  521.3 5.1 fusion.163
  528.0 5.1 fusion.163
  534.7 5.1 fusion.163
  548.2 5.1 fusion.163
  553.3 24.2 %reduce-scatter.5.cloned.1.call-done = f32[32,8,256]{2,1,0:T(8,128)} async-done(((f32[128,8,256]{2,1,0:T(8,128)}), f32[32,8,256]{2,1,0:T(8,128)}) %reduce-scatter.5.cloned.1.call-update) | async-done | bytes 262160 | tf_op jit(solution)/shard_map/reduce_scatter | solution.py:214
  (360 shorter events, 293.8 us)
Async XLA Ops:
  6.5 2.6 copy-start
  22.8 10.1 %copy-start.5 = (s32[2]{0:T(128)S(1)}, s32[2]{0:T(128)}, u32[]{:S(2)}) copy-start(s32[2]{0:T(128)} %param.14) | copy-start | bytes 28
  22.8 11.9 %copy-start.6 = (s32[2,8]{1,0:T(2,128)S(1)}, s32[2,8]{1,0:T(2,128)}, u32[]{:S(2)}) copy-start(s32[2,8]{1,0:T(2,128)} %param.15) | copy-start | bytes 196
  22.8 100.7 %all-to-all-start = ((bf16[128,4,4096]{2,1,0:T(4,128)(2,1)}), bf16[128,4,4096]{2,1,0:T(4,128)(2,1)}, u32[]{:S(2)}, u32[]{:S(2)}) async-start(bf16[128,4,4096]{2,1,0:T(4,128)(2,1)} %select_select_fusion.1), calls=%async_computation | async-start | bytes 8388608 | tf_op jit(solution)/shard_map/all_to_all | solution.py:201
  30.2 312.4 %all-reduce.4.cloned.1.call-start = ((), (), s32[]{:S(2)}) async-start(), calls=%async_computation.5 | async-start | bytes 1048576 | tf_op jit(solution)/shard_map/psum | solution.py:22
  154.9 1.2 copy-start.2
  168.8 1.2 copy-start.2
  182.8 1.2 copy-start.2
  196.7 1.2 copy-start.2
  210.7 1.2 copy-start.2
  224.6 1.2 copy-start.2
  238.5 1.2 copy-start.2
  252.4 1.2 copy-start.2
  262.7 8.0 %copy-start.3 = (f32[2048,256]{1,0:T(8,128)S(1)}, f32[2048,256]{1,0:T(8,128)}, u32[]{:S(2)}) copy-start(f32[2048,256]{1,0:T(8,128)} %get-tuple-element.333) | copy-start | bytes 6291460
  270.6 282.7 %reduce-scatter.3.cloned.1.call-start = ((), (), s32[]{:S(2)}) async-start(), calls=%async_computation.3 | async-start | bytes 1310720 | tf_op jit(solution)/shard_map/reduce_scatter | solution.py:214
  442.0 1.1 copy-start.4
  443.1 134.4 %reduce-scatter.5.cloned.1.call-start = ((), (), s32[]{:S(2)}) async-start(), calls=%async_computation.4 | async-start | bytes 1310720 | tf_op jit(solution)/shard_map/reduce_scatter | solution.py:214
  553.3 26.1 %copy-start.1 = (bf16[64,4,4096]{2,1,0:T(4,128)(2,1)S(1)}, bf16[64,4,4096]{2,1,0:T(4,128)(2,1)}, u32[]{:S(2)}) copy-start(bf16[64,4,4096]{2,1,0:T(4,128)(2,1)} %param.12) | copy-start | bytes 6291460
Sparse Core Ops, SparseCore 0:
  270.7 71.8 all-reduce.3
  443.2 23.9 reduce-scatter.2
  553.4 24.0 reduce-scatter.4
where the time goes:
time: 590 us; the launch traced here: 586 us
  matrix products  193 us (33%)
  waiting for transfers between devices  164 us (28%)
  local copies, waits for them, and re-layouts  119 us (20%)
  other arithmetic  87.6 us (15%)
  between operations  14.6 us (2%)
  starting transfers between devices  7.53 us (1%)
    dot_general x32, matrix products, one_group(): jnp.einsum('nvk,kl->nvl', stacked, inverse_table, precision=lax.Precision...  152 us
    all_to_all x1, waiting for transfers between devices, body(): lax.all_to_all(outgoing, 'chan', split_axis=0, concat_axis=0, tiled=True)  78.6 us
    psum x1, waiting for transfers between devices, spread(): return lax.psum(kept, axis)  60.8 us
    squeeze x32, local copies, waits for them, and re-layouts, correlate(): result = lax.map(one_group, grouped)  33.4 us
    reduce_scatter x2, waiting for transfers between devices, body(): lax.psum_scatter(stack_term(jnp.int32(0), slot_share * lax.axis_size('tm'...  24.2 us
    convert_element_type x16, local copies, waits for them, and re-layouts, whiten_block(): row_block.astype(jnp.float32) * window_taper  21.4 us
    dot_general x8, matrix products, whiten_block(): jnp.einsum('ntk,tj->njk', turned, second_table, precision=lax.Precision.H...  20.9 us
    reduce_sum x32, other arithmetic, one_group(): jnp.sum(block_real * source_real[None] + block_imag * source_imag[None],...  18.1 us
  transfers between devices with their start and end apart: 4, of which 3 were waited for; matrix products, arithmetic and copies ran while one was open for 23% of the time, Pallas kernels for 0%

commit v1 on v0

v1 whole, which is shorter than its diff:
```python
import functools
import math

import jax
import jax.numpy as jnp
import numpy as np
from jax import lax
from jax.experimental import pallas as pl
from jax.experimental.pallas import tpu as pltpu
from jax.sharding import PartitionSpec as P

L = 4096
HALF = L // 2
HW = 64
LAGS = 256
EPSILON = 1e-06
TB = 16
TA = L // TB
KA = HALF // TB


def make_tables():
    a = np.arange(TA, dtype=np.int64)
    taper = 0.5 - 0.5 * np.cos(2 * np.pi / L * (np.arange(L) + 0.5))
    kb = np.arange(TB // 2 + 1, dtype=np.int64)
    twist = 2 * np.pi / L * (kb[:, None] * a[None, :])
    twist_cos, twist_sin = np.cos(twist), np.sin(twist)
    ka = np.arange(KA, dtype=np.int64)
    low = 2 * np.pi / TA * (a[:, None] * ka[None, :] % TA)
    high = 2 * np.pi / TA * (a[:, None] * (TA - 1 - ka)[None, :] % TA)
    top = [np.cos(low), -np.sin(low), np.cos(high), np.sin(high)]
    bottom = [np.sin(low), np.cos(low), np.sin(high), -np.cos(high)]
    second = np.concatenate([np.concatenate(top, 1), np.concatenate(bottom, 1)], 0)
    bins = np.arange(TB)[:, None] + TB * ka[None, :]
    counts = np.minimum(bins, HW) + np.minimum(HALF - 1 - bins, HW) + 1
    lag = np.arange(LAGS, dtype=np.int64) - LAGS // 2
    angle = 2 * np.pi / L * (bins[:, :, None] * lag % L)
    weight = np.where(bins == 0, 1.0, 2.0)[:, :, None]
    inverse = np.stack([weight * np.cos(angle), -weight * np.sin(angle)], 1)
    f32 = np.float32
    return (
        taper.astype(f32)[None, :],
        twist_cos.astype(f32),
        twist_sin.astype(f32),
        second.astype(jnp.bfloat16),
        (1.0 / counts).astype(f32),
        inverse.reshape(L, LAGS).astype(jnp.bfloat16),
    )


def dft4(x0, x1, x2, x3):
    if x0[1] is None:
        s, d = x0[0] + x2[0], x0[0] - x2[0]
        u, v = x1[0] + x3[0], x1[0] - x3[0]
        return (s + u, None), (d, -v), (s - u, None), (d, v)
    sr, si, dr, di = x0[0] + x2[0], x0[1] + x2[1], x0[0] - x2[0], x0[1] - x2[1]
    ur, ui, vr, vi = x1[0] + x3[0], x1[1] + x3[1], x1[0] - x3[0], x1[1] - x3[1]
    return (sr + ur, si + ui), (dr + vi, di - vr), (sr - ur, si - ui), (dr - vi, di + vr)


def turn(value, step):
    c, s = math.cos(2 * math.pi * step / TB), math.sin(2 * math.pi * step / TB)
    re, im = value
    if step == 0:
        return value
    if im is None:
        return re * c, re * (-s)
    return re * c + im * s, im * c - re * s


def dft16_real(x):
    first = [dft4(*[(x[n + 4 * m], None) for m in range(4)]) for n in range(4)]
    out = [None] * 9
    for q in range(3):
        parts = [turn(first[n][q], n * q) for n in range(4)]
        if q == 0:
            r = [p[0] for p in parts]
            out[0] = (r[0] + r[1] + r[2] + r[3], None)
            out[4] = (r[0] - r[2], r[3] - r[1])
            out[8] = ((r[0] + r[2]) - (r[1] + r[3]), None)
        else:
            if parts[0][1] is None:
                parts[0] = (parts[0][0], jnp.zeros_like(parts[0][0]))
            y = dft4(*parts)
            out[q] = y[0]
            out[q + 4] = y[1]
            if q == 1:
                out[3] = (y[3][0], -y[3][1])
            else:
                pass
    parts = [turn(first[n][1], n) for n in range(4)]
    y = dft4(*parts)
    out[7] = (y[2][0], -y[2][1])
    return out


def whiten_kernel(x_ref, taper_ref, cos_ref, sin_ref, second_ref, count_ref, o_ref, turned, spec):
    rows = x_ref.shape[0]
    place = {q: (q - 1) * rows for q in range(1, 9)}
    place[0] = 8 * rows
    group = 16

    @pl.loop(0, rows // group)
    def _(step):
        base = pl.multiple_of(step * group, group)
        for h in range(TA // 128):
            x = []
            for b in range(TB):
                cols = pl.ds(b * TA + h * 128, 128)
                v = x_ref[pl.ds(base, group), cols].astype(jnp.float32) * taper_ref[:, cols]
                x.append(v.astype(jnp.bfloat16).astype(jnp.float32))
            y = dft16_real(x)
            here = pl.ds(h * 128, 128)
            there = pl.ds(TA + h * 128, 128)
            for q in range(TB // 2 + 1):
                re, im = y[q]
                target = pl.ds(pl.multiple_of(base + place[q], group), group)
                if q == 0:
                    out_re, out_im = re, jnp.zeros_like(re)
                else:
                    c, s = cos_ref[pl.ds(q, 1), here], sin_ref[pl.ds(q, 1), here]
                    if im is None:
                        out_re, out_im = re * c, -(re * s)
                    else:
                        out_re, out_im = re * c + im * s, im * c - re * s
                turned[target, here] = out_re.astype(jnp.bfloat16)
                turned[target, there] = out_im.astype(jnp.bfloat16)

    split = 7 * rows
    spec[0:split, :] = jnp.dot(
        turned[0:split, :], second_ref[...], preferred_element_type=jnp.float32
    )
    spec[split:, 0 : 2 * KA] = jnp.dot(
        turned[split:, :], second_ref[:, 0 : 2 * KA], preferred_element_type=jnp.float32
    )

    lane = lax.broadcasted_iota(jnp.int32, (8, KA), 1)

    def ahead(v, d):
        return jnp.where(lane < KA - d, pltpu.roll(v, KA - d, 1), 0.0)

    def behind(v, d):
        return jnp.where(lane >= d, pltpu.roll(v, d, 1), 0.0)

    @pl.loop(0, rows // 16)
    def _(step):
        done = [[], []]
        for half in range(2):
            base = pl.multiple_of(step * 16, 16) + half * 8

            def part(q, imag):
                src, col = (q, 0) if q <= 8 else (TB - q, 2 * KA)
                at = pl.ds(pl.multiple_of(base + place[src], 8), 8)
                return spec[at, pl.ds(col + imag * KA, KA)]

            mags = []
            for q in range(TB):
                re, im = part(q, 0), part(q, 1)
                m = jnp.sqrt(re * re + im * im)
                mags.append(m.astype(jnp.bfloat16).astype(jnp.float32))
            prefix = [mags[0]]
            for q in range(1, TB):
                prefix.append(prefix[-1] + mags[q])
            total = prefix[-1]
            near = total
            for d in (1, 2, 3):
                near = near + ahead(total, d) + behind(total, d)
            suffix = total
            for q in range(TB):
                smooth = near + behind(suffix, 4) + ahead(prefix[q], 4)
                suffix = suffix - mags[q]
                inv = 1.0 / (smooth * count_ref[pl.ds(q, 1), :] + EPSILON)
                done[half].append((part(q, 0) * inv, part(q, 1) * inv))
        at = pl.ds(pl.multiple_of(step * 16, 16), 16)
        for q in range(TB):
            for p in range(2):
                both = jnp.concatenate([done[0][q][p], done[1][q][p]], axis=0)
                o_ref[at, pl.ds(q * 2 * KA + p * KA, KA)] = both.astype(jnp.bfloat16)


def whiten(rows_by_window, tables):
    rows = rows_by_window.shape[0]
    windows = rows_by_window.shape[1] // L
    taper, tcos, tsin, second, rcount, _ = tables
    full = lambda v: pl.BlockSpec(v.shape, lambda w: (0, 0))
    flops = 2 * 9 * rows * windows * 512 * 512
    return pl.pallas_call(
        whiten_kernel,
        grid=(windows,),
        in_specs=[pl.BlockSpec((rows, L), lambda w: (0, w))]
        + [full(v) for v in (taper, tcos, tsin, second, rcount)],
        out_specs=pl.BlockSpec((rows, L), lambda w: (w, 0)),
        out_shape=jax.ShapeDtypeStruct((windows * rows, L), jnp.bfloat16),
        scratch_shapes=[
            pltpu.VMEM((9 * rows, 2 * TA), jnp.bfloat16),
            pltpu.VMEM((9 * rows, 4 * KA), jnp.float32),
        ],
        cost_estimate=pl.CostEstimate(
            flops=flops, bytes_accessed=4 * rows * windows * L, transcendentals=0
        ),
        name="whiten",
    )(rows_by_window, taper, tcos, tsin, second, rcount)


def correlate_kernel(windows, sources, scale, own_ref, src_ref, inv_ref, o_ref, cross):
    chans = own_ref.shape[0] // windows

    @pl.loop(0, TB)
    def _(q):
        col_re = pl.ds(pl.multiple_of(q * 2 * KA, KA), KA)
        col_im = pl.ds(pl.multiple_of(q * 2 * KA + KA, KA), KA)
        for n in range(sources):
            s_re = [
                jnp.broadcast_to(src_ref[pl.ds(w * sources + n, 1), col_re], (16, KA)).astype(jnp.float32)
                for w in range(windows)
            ]
            s_im = [
                jnp.broadcast_to(src_ref[pl.ds(w * sources + n, 1), col_im], (16, KA)).astype(jnp.float32)
                for w in range(windows)
            ]
            for g in range(chans // 16):
                re = im = None
                for w in range(windows):
                    at = pl.ds(w * chans + g * 16, 16)
                    a = own_ref[at, col_re].astype(jnp.float32)
                    b = own_ref[at, col_im].astype(jnp.float32)
                    r = a * s_re[w] + b * s_im[w]
                    i = b * s_re[w] - a * s_im[w]
                    re = r if re is None else re + r
                    im = i if im is None else im + i
                at = pl.ds(n * chans + g * 16, 16)
                cross[at, col_re] = re.astype(jnp.bfloat16)
                cross[at, col_im] = im.astype(jnp.bfloat16)

    tile = math.gcd(sources * chans, 256)

    @pl.loop(0, sources * chans // tile)
    def _(step):
        at = pl.ds(pl.multiple_of(step * tile, tile), tile)
        out = jnp.dot(cross[at, :], inv_ref[...], preferred_element_type=jnp.float32)
        o_ref[at, :] = (out * scale).astype(jnp.bfloat16)


def correlate(own, src, windows, scale, tables):
    chans, sources = own.shape[0] // windows, src.shape[0] // windows
    inverse = tables[5]
    whole = pl.BlockSpec(memory_space=pltpu.VMEM)
    return pl.pallas_call(
        functools.partial(correlate_kernel, windows, sources, scale),
        in_specs=[whole] * 3,
        out_specs=whole,
        out_shape=jax.ShapeDtypeStruct((sources * chans, LAGS), jnp.bfloat16),
        scratch_shapes=[pltpu.VMEM((sources * chans, L), jnp.bfloat16)],
        name="correlate",
    )(own, src, inverse)


def body(raw_traces, owner_lists, source_owner, source_slot):
    block, windows, length = raw_traces.shape
    owners = lax.axis_size("chan")
    shards = lax.axis_size("tm")
    capacity = owner_lists.shape[1]
    slots = (capacity + owners - 1) // owners
    share = capacity // shards
    me = lax.axis_index("chan")
    tables = tuple(jnp.asarray(t) for t in make_tables())
    scale = 1.0 / math.sqrt(windows * shards * HALF)
    bf16, f32 = jnp.bfloat16, jnp.float32

    traces = raw_traces.reshape(block, windows * length)
    ids = owner_lists[source_owner[:, None], source_slot].reshape(-1)
    sources = ids.shape[0]
    pick = (ids[:, None] == me * block + jnp.arange(block)[None, :]).astype(bf16)
    mine = jnp.dot(pick, traces, preferred_element_type=f32).astype(bf16)
    source_rows = lax.psum(mine, "chan")

    own = whiten(traces, tables)
    src = whiten(source_rows, tables)
    partial = correlate(own, src, windows, scale, tables)

    per = sources // shards
    parts = lax.all_to_all(
        partial.reshape(shards, per, block, LAGS), "tm", split_axis=0, concat_axis=0, tiled=True
    )
    summed = jnp.sum(parts.astype(f32), axis=0).astype(bf16)

    source_block = jnp.floor_divide(owner_lists, block)
    matched = (owner_lists >= 0) & (source_block == me)
    rank = jnp.cumsum(matched.astype(jnp.int32), axis=1) - 1
    slot_ids = jnp.arange(slots, dtype=jnp.int32)
    chosen = matched[:, None, :] & (rank[:, None, :] == slot_ids[None, :, None])
    wanted = jnp.sum(jnp.where(chosen, owner_lists[:, None, :] - me * block + 1, 0), axis=2) - 1
    send = (wanted[:, :, None] == jnp.arange(block)[None, None, :]).astype(bf16)
    outgoing = jnp.einsum("osc,ncl->onsl", send, summed, preferred_element_type=f32).astype(bf16)
    arrived = lax.all_to_all(outgoing, "chan", split_axis=0, concat_axis=0, tiled=True)

    my_list = lax.dynamic_index_in_dim(owner_lists, me, 0, keepdims=False)
    my_block = jnp.floor_divide(my_list, block)
    live = my_list >= 0
    position = jnp.arange(capacity, dtype=jnp.int32)
    same = (my_block[:, None] == my_block[None, :]) & (position[None, :] < position[:, None]) & live[None, :]
    earlier = jnp.sum(same.astype(jnp.int32), axis=1)
    take = (
        live[:, None, None]
        & (my_block[:, None, None] == jnp.arange(owners)[None, :, None])
        & (earlier[:, None, None] == slot_ids[None, None, :])
    ).astype(bf16)
    placed = jnp.einsum("rcs,cnsl->rnl", take, arrived, preferred_element_type=f32).astype(bf16)
    result = lax.all_to_all(placed, "tm", split_axis=0, concat_axis=1, tiled=True)
    return result.astype(f32)


def solution(mesh):
    return jax.shard_map(
        body,
        mesh=mesh,
        in_specs=(P("chan", "tm", None), P(), P(), P()),
        out_specs=P(("chan", "tm"), None, None),
        check_vma=False,
    )
```

time: 590 us -> 151 us (0.26)
  matrix products: 193 us -> 1.79 us
  local copies, waits for them, and re-layouts: 119 us -> 5.56 us
  other arithmetic: 87.6 us -> 0.97 us
  waiting for transfers between devices: 164 us -> 83 us
  Pallas kernels: 0 us -> 30.5 us
  blocking collectives: 0 us -> 8.39 us
    dot_general x56 -> x3, matrix products: 193 us -> 1.79 us  [the longest x1 1.26 us: body(): mine = jnp.dot(pick, traces, preferred_element_type=f32).astype(bf16)]
    all_to_all x1, waiting for transfers between devices: 78.6 us -> 8.42 us  [body(): lax.all_to_all(outgoing, 'chan', split_axis=0, concat_axis=0, tiled=True)]
    squeeze x33 -> x0, local copies, waits for them, and re-layouts: 33.5 us -> none  [the longest x32 33.4 us: correlate(): result = lax.map(one_group, grouped)]
    pallas_call x0 -> x3, Pallas kernels: none -> 30.5 us  [the longest x1 17 us: correlate(): pl.pallas_call(functools.partial(correlate_kernel, windows, sources, scal...]
    gather x5 -> x1, local copies, waits for them, and re-layouts: 30.2 us -> 0.64 us  [body(): ids = owner_lists[source_owner[:, None], source_slot].reshape(-1)]
    reduce_scatter x2 -> x0, waiting for transfers between devices: 24.2 us -> none  [body(): lax.psum_scatter(stack_term(jnp.int32(0), slot_share * lax.axis_size('tm'...]
    convert_element_type x24 -> x4, local copies, waits for them, and re-layouts: 23.4 us -> 1.97 us  [the longest x2 1.04 us: body(): return result.astype(f32)]
    reduce_sum x34 -> x3, other arithmetic: 18.5 us -> 0.46 us  [the longest x1 0.21 us: body(): jnp.sum(jnp.where(chosen, owner_lists[:, None, :] - me * block + 1, 0), a...]
  transfers between devices with their start and end apart: 4 -> 3, of which waited for: 3 -> 3; matrix products, arithmetic and copies ran while one was open for 23% -> 0% of each run, Pallas kernels for 0% -> 6%
where the time goes in v1:
time: 151 us
  waiting for transfers between devices  83 us (55%)
  Pallas kernels  30.5 us (20%)
  between operations  13.6 us (9%)
  blocking collectives  8.39 us (6%)
  starting transfers between devices  7.26 us (5%)
  local copies, waits for them, and re-layouts  5.56 us (4%)
  matrix products  1.79 us (1%)
    psum x1, waiting for transfers between devices, body(): source_rows = lax.psum(mine, 'chan')  66 us
    pallas_call x1, Pallas kernels, correlate(): pl.pallas_call(functools.partial(correlate_kernel, windows, sources, scal...  17 us
    pallas_call x2, Pallas kernels, whiten(): pl.pallas_call(whiten_kernel, grid=(windows,), in_specs=[pl.BlockSpec((ro...  13.5 us
    all_to_all x1, waiting for transfers between devices, body(): lax.all_to_all(partial.reshape(shards, per, block, LAGS), 'tm', split_axi...  8.54 us
    all_to_all x1, waiting for transfers between devices, body(): lax.all_to_all(outgoing, 'chan', split_axis=0, concat_axis=0, tiled=True)  8.42 us
    all_to_all x1, blocking collectives, body(): lax.all_to_all(placed, 'tm', split_axis=0, concat_axis=1, tiled=True)  8.39 us
    all_to_all x1, starting transfers between devices, body(): lax.all_to_all(outgoing, 'chan', split_axis=0, concat_axis=0, tiled=True)  3.78 us
    all_to_all x1, starting transfers between devices, body(): lax.all_to_all(partial.reshape(shards, per, block, LAGS), 'tm', split_axi...  3.47 us
  transfers between devices with their start and end apart: 3, of which 3 were waited for; matrix products, arithmetic and copies ran while one was open for 0% of the time, Pallas kernels for 6%

profile of v1, /device:TPU:0, one launch (start us, length us, event | category | flops | bytes accessed | tf_op | source)
XLA Modules:
  0.0 151.0 jit_solution(1675716901516622187)
XLA Ops:
  6.5 2.9 %copy.23 = bf16[8,8,4,4096]{3,1,2,0:T(8,128)(2,1)S(1)} copy(bf16[8,8,4,4096]{3,2,1,0:T(4,128)(2,1)} %bitcast.53) | data formatting | bytes 4194304
  9.5 0.1 fusion.23
  9.5 0.1 reshape.163
  9.6 0.6 gather_fusion
  10.3 1.3 convolution_convert_fusion
  11.6 0.3 reduce_window_sum.11
  11.9 9.2 %whiten.2.own_ref = bf16[256,4096]{1,0:T(8,128)(2,1)} custom-call(bf16[64,16384]{1,0:T(8,128)(2,1)} %bitcast.51, f32[1,4096]{1,0:T(1,128)} %constant.68.clone.taper_ref, f32[9,256]{1,0:T(8,128)} %constant.69.clone.cos_ref, f32[9,256]{1,0:T(8,128)} %constant.70.clone.sin_ref, bf16[512,512]{1,0:T(8,128)(2,1)} %constant.71.clone.second_ref, ...), custom_call_target="tpu_custom_call" | custom-call | flops 1207959552 | bytes 4194304 | tf_op jit(solution)/shard_map/whiten/pallas_call | solution.py:187
  21.1 66.0 %all-reduce.2.cloned.1.call-done.x_ref = bf16[16,16384]{1,0:T(8,128)(2,1)} async-done(((bf16[16,16384]{1,0:T(8,128)(2,1)}), bf16[16,16384]{1,0:T(8,128)(2,1)}) %all-reduce.2.cloned.1.call-update) | async-done | bytes 524304 | tf_op jit(solution)/shard_map/psum | solution.py:275
  87.1 4.3 %whiten.3.src_ref = bf16[64,4096]{1,0:T(8,128)(2,1)} custom-call(bf16[16,16384]{1,0:T(8,128)(2,1)} %all-reduce.2.cloned.1.call-done.x_ref, f32[1,4096]{1,0:T(1,128)} %constant.68.clone.taper_ref, f32[9,256]{1,0:T(8,128)} %constant.69.clone.cos_ref, f32[9,256]{1,0:T(8,128)} %constant.70.clone.sin_ref, bf16[512,512]{1,0:T(8,128)(2,1)} %constant.71.clone.second_ref, ...), custom_call_target="tpu_custom_call" | custom-call | flops 301989888 | bytes 1048576 | tf_op jit(solution)/shard_map/whiten/pallas_call | solution.py:187
  91.4 17.0 %correlate.1 = bf16[1024,256]{1,0:T(8,128)(2,1)} custom-call(bf16[256,4096]{1,0:T(8,128)(2,1)} %whiten.2.own_ref, bf16[64,4096]{1,0:T(8,128)(2,1)} %whiten.3.src_ref, bf16[4096,256]{1,0:T(8,128)(2,1)} %constant.73.clone.inv_ref), custom_call_target="tpu_custom_call" | custom-call | tf_op jit(solution)/shard_map/correlate/pallas_call | solution.py:248
  108.4 3.5 %all-to-all-start = ((bf16[4,4,64,256]{3,2,1,0:T(8,128)(2,1)}), bf16[4,4,64,256]{3,2,1,0:T(8,128)(2,1)S(1)}, u32[]{:S(2)}, u32[]{:S(2)}) async-start(bf16[4,4,64,256]{3,2,1,0:T(8,128)(2,1)} %bitcast.52), calls=%async_computation | async-start | bytes 1048576 | tf_op jit(solution)/shard_map/all_to_all | solution.py:282
  111.9 0.2 select_reduce_fusion
  112.1 8.5 %all-to-all-done = bf16[4,4,64,256]{3,2,1,0:T(8,128)(2,1)S(1)} async-done(((bf16[4,4,64,256]{3,2,1,0:T(8,128)(2,1)}), bf16[4,4,64,256]{3,2,1,0:T(8,128)(2,1)S(1)}, u32[]{:S(2)}, u32[]{:S(2)}) %all-to-all-start) | async-done | bytes 524320 | tf_op jit(solution)/shard_map/all_to_all | solution.py:282
  120.6 0.1 reduce_sum.31
  120.7 0.3 fusion.1
  121.0 0.7 copy.17
  121.7 3.8 %all-to-all-start.1 = ((bf16[8,4,16,256]{3,2,1,0:T(8,128)(2,1)}), bf16[8,4,16,256]{3,2,1,0:T(8,128)(2,1)S(1)}, u32[]{:S(2)}, u32[]{:S(2)}) async-start(bf16[8,4,16,256]{3,2,1,0:T(8,128)(2,1)} %copy.17), calls=%async_computation.1 | async-start | bytes 524288 | tf_op jit(solution)/shard_map/all_to_all | solution.py:295
  125.5 0.2 convert_reduce_fusion
  125.7 8.4 %all-to-all-done.1 = bf16[8,4,16,256]{3,2,1,0:T(8,128)(2,1)S(1)} async-done(((bf16[8,4,16,256]{3,2,1,0:T(8,128)(2,1)}), bf16[8,4,16,256]{3,2,1,0:T(8,128)(2,1)S(1)}, u32[]{:S(2)}, u32[]{:S(2)}) %all-to-all-start.1) | async-done | bytes 262176 | tf_op jit(solution)/shard_map/all_to_all | solution.py:295
  134.1 0.3 fusion
  134.4 0.2 copy.19
  134.6 8.4 %all_to_all.19 = bf16[128,4,256]{2,1,0:T(4,128)(2,1)S(1)} all-to-all(bf16[128,4,256]{2,1,0:T(4,128)(2,1)S(1)} %copy.19), channel_id=1, replica_groups=mesh['chan'=8,'tm'=4] {'tm'}, dimensions={0} | all-to-all | bytes 524288 | tf_op jit(solution)/shard_map/all_to_all | solution.py:309
  143.0 0.1 convert_bitcast_fusion
  143.2 1.0 reshape.161
  (23 shorter events, 0.2 us)
Async XLA Ops:
  6.5 80.6 %all-reduce.2.cloned.1.call-start = ((), (), s32[]{:S(2)}) async-start(), calls=%async_computation.3 | async-start | bytes 1048576 | tf_op jit(solution)/shard_map/psum | solution.py:275
  6.5 2.9 %copy-start.3 = (s32[2]{0:T(128)S(1)}, s32[2]{0:T(128)}, u32[]{:S(2)}) copy-start(s32[2]{0:T(128)} %param.12) | copy-start | bytes 28
  6.5 2.9 %copy-start.2 = (s32[2,8]{1,0:T(2,128)S(1)}, s32[2,8]{1,0:T(2,128)}, u32[]{:S(2)}) copy-start(s32[2,8]{1,0:T(2,128)} %param.13) | copy-start | bytes 196
  6.5 3.1 %copy-start = (s32[8,128]{1,0:T(8,128)S(1)}, s32[8,128]{1,0:T(8,128)}, u32[]{:S(2)}) copy-start(s32[8,128]{1,0:T(8,128)} %param.11) | copy-start | bytes 12292
  9.4 2.1 %copy-start.1 = (bf16[8,8,4,4096]{3,1,2,0:T(8,128)(2,1)}, bf16[8,8,4,4096]{3,1,2,0:T(8,128)(2,1)S(1)}, u32[]{:S(2)}) copy-start(bf16[8,8,4,4096]{3,1,2,0:T(8,128)(2,1)S(1)} %copy.23) | copy-start | bytes 6291460
  108.4 12.3 %all-to-all-start = ((bf16[4,4,64,256]{3,2,1,0:T(8,128)(2,1)}), bf16[4,4,64,256]{3,2,1,0:T(8,128)(2,1)S(1)}, u32[]{:S(2)}, u32[]{:S(2)}) async-start(bf16[4,4,64,256]{3,2,1,0:T(8,128)(2,1)} %bitcast.52), calls=%async_computation | async-start | bytes 1048576 | tf_op jit(solution)/shard_map/all_to_all | solution.py:282
  121.7 12.4 %all-to-all-start.1 = ((bf16[8,4,16,256]{3,2,1,0:T(8,128)(2,1)}), bf16[8,4,16,256]{3,2,1,0:T(8,128)(2,1)S(1)}, u32[]{:S(2)}, u32[]{:S(2)}) async-start(bf16[8,4,16,256]{3,2,1,0:T(8,128)(2,1)} %copy.17), calls=%async_computation.1 | async-start | bytes 524288 | tf_op jit(solution)/shard_map/all_to_all | solution.py:295
Sparse Core Ops, SparseCore 0:
  11.7 75.3 all-reduce.1

commit v2 on v1

--- a/solution.py
+++ b/solution.py
@@ -94,8 +94,9 @@
     return out
 
 
-def whiten_kernel(x_ref, taper_ref, cos_ref, sin_ref, second_ref, count_ref, o_ref, turned, spec):
-    rows = x_ref.shape[0]
+def whiten_rows(load, store, tables, turned, spec):
+    taper_ref, cos_ref, sin_ref, second_ref, count_ref = tables
+    rows = turned.shape[0] // 9
     place = {q: (q - 1) * rows for q in range(1, 9)}
     place[0] = 8 * rows
     group = 16
@@ -107,7 +108,7 @@
             x = []
             for b in range(TB):
                 cols = pl.ds(b * TA + h * 128, 128)
-                v = x_ref[pl.ds(base, group), cols].astype(jnp.float32) * taper_ref[:, cols]
+                v = load(step, b * TA + h * 128).astype(jnp.float32) * taper_ref[:, cols]
                 x.append(v.astype(jnp.bfloat16).astype(jnp.float32))
             y = dft16_real(x)
             here = pl.ds(h * 128, 128)
@@ -171,35 +172,214 @@
                 suffix = suffix - mags[q]
                 inv = 1.0 / (smooth * count_ref[pl.ds(q, 1), :] + EPSILON)
                 done[half].append((part(q, 0) * inv, part(q, 1) * inv))
-        at = pl.ds(pl.multiple_of(step * 16, 16), 16)
         for q in range(TB):
             for p in range(2):
                 both = jnp.concatenate([done[0][q][p], done[1][q][p]], axis=0)
-                o_ref[at, pl.ds(q * 2 * KA + p * KA, KA)] = both.astype(jnp.bfloat16)
-
-
-def whiten(rows_by_window, tables):
-    rows = rows_by_window.shape[0]
-    windows = rows_by_window.shape[1] // L
+                store(step, q * 2 * KA + p * KA, both.astype(jnp.bfloat16))
+
+
+def partners(axis, extent):
+    me = lax.axis_index(axis)
+    return me, [lax.rem(me + k, extent) for k in range(extent)]
+
+
+def remote(src, dst, send, recv, axis, device):
+    return pltpu.make_async_remote_copy(
+        src_ref=src,
+        dst_ref=dst,
+        send_sem=send,
+        recv_sem=recv,
+        device_id={axis: device},
+        device_id_type=pl.DeviceIdType.MESH,
+    )
+
+
+def greet(pairs):
+    barrier = pltpu.get_barrier_semaphore()
+    for axis, device in pairs:
+        pl.semaphore_signal(
+            barrier, inc=1, device_id={axis: device}, device_id_type=pl.DeviceIdType.MESH
+        )
+    pl.semaphore_wait(barrier, len(pairs))
+
+
+def whiten_kernel(
+    owners, windows, traces_ref, mine_ref, taper_ref, cos_ref, sin_ref, second_ref, count_ref,
+    own_ref, src_ref, turned, spec, shares, piece, rows_all, send_a, recv_a, send_b, recv_b,
+):
+    tables = (taper_ref, cos_ref, sin_ref, second_ref, count_ref)
+    rows = traces_ref.shape[0]
+    width = traces_ref.shape[1] // owners
+    me, others = partners("chan", owners)
+    greet([("chan", others[k]) for k in range(1, owners)])
+
+    def cut(device):
+        return pl.ds(pl.multiple_of(device * width, 128), width)
+
+    def first(k):
+        return remote(
+            mine_ref.at[:, cut(others[k])], shares.at[k], send_a.at[k], recv_a.at[k], "chan", others[k]
+        )
+
+    def second(k):
+        return remote(piece, rows_all.at[:, cut(me)], send_b.at[k], recv_b.at[k], "chan", others[k])
+
+    for k in range(1, owners):
+        first(k).start()
+
+    @pl.loop(0, windows)
+    def _(w):
+        @pl.when(w == windows // 2)
+        def _():
+            total = mine_ref[:, cut(me)].astype(jnp.float32)
+            for k in range(1, owners):
+                first(k).wait()
+                total = total + shares[k].astype(jnp.float32)
+            piece[...] = total.astype(jnp.bfloat16)
+            rows_all[:, cut(me)] = total.astype(jnp.bfloat16)
+            for k in range(1, owners):
+                second(k).start()
+
+        def load(step, col):
+            at = pl.ds(pl.multiple_of(step * 16, 16), 16)
+            return traces_ref[at, pl.ds(pl.multiple_of(w * L + col, 128), 128)]
+
+        def store(step, col, value):
+            at = pl.ds(pl.multiple_of(w * rows + step * 16, 16), 16)
+            own_ref[at, pl.ds(col, KA)] = value
+
+        whiten_rows(load, store, tables, turned, spec)
+
+    for k in range(1, owners):
+        second(k).wait()
+
+    def load(step, col):
+        return rows_all[:, pl.ds(pl.multiple_of(step * L + col, 128), 128)]
+
+    def store(step, col, value):
+        src_ref[pl.ds(pl.multiple_of(step * 16, 16), 16), pl.ds(col, KA)] = value
+
+    few = windows * rows_all.shape[0]
+    whiten_rows(load, store, tables, turned.at[0 : 9 * few, :], spec.at[0 : 9 * few, :])
+
+
+def whiten(traces, mine, owners, windows, tables):
+    rows, sources = traces.shape[0], mine.shape[0]
     taper, tcos, tsin, second, rcount, _ = tables
-    full = lambda v: pl.BlockSpec(v.shape, lambda w: (0, 0))
-    flops = 2 * 9 * rows * windows * 512 * 512
+    whole = pl.BlockSpec(memory_space=pltpu.VMEM)
+    most = max(rows, windows * sources)
+    width = windows * L // owners
+    bf16 = jnp.bfloat16
     return pl.pallas_call(
-        whiten_kernel,
-        grid=(windows,),
-        in_specs=[pl.BlockSpec((rows, L), lambda w: (0, w))]
-        + [full(v) for v in (taper, tcos, tsin, second, rcount)],
-        out_specs=pl.BlockSpec((rows, L), lambda w: (w, 0)),
-        out_shape=jax.ShapeDtypeStruct((windows * rows, L), jnp.bfloat16),
+        functools.partial(whiten_kernel, owners, windows),
+        in_specs=[whole] * 7,
+        out_specs=[whole] * 2,
+        out_shape=[
+            jax.ShapeDtypeStruct((windows * rows, L), bf16),
+            jax.ShapeDtypeStruct((windows * sources, L), bf16),
+        ],
         scratch_shapes=[
-            pltpu.VMEM((9 * rows, 2 * TA), jnp.bfloat16),
-            pltpu.VMEM((9 * rows, 4 * KA), jnp.float32),
-        ],
-        cost_estimate=pl.CostEstimate(
-            flops=flops, bytes_accessed=4 * rows * windows * L, transcendentals=0
-        ),
+            pltpu.VMEM((9 * most, 2 * TA), bf16),
+            pltpu.VMEM((9 * most, 4 * KA), jnp.float32),
+            pltpu.VMEM((owners, sources, width), bf16),
+            pltpu.VMEM((sources, width), bf16),
+            pltpu.VMEM((sources, windows * L), bf16),
+        ]
+        + [pltpu.SemaphoreType.DMA((owners,))] * 4,
+        compiler_params=pltpu.CompilerParams(collective_id=0, has_side_effects=True),
         name="whiten",
-    )(rows_by_window, taper, tcos, tsin, second, rcount)
+    )(traces, mine, taper, tcos, tsin, second, rcount)
+
+
+def deliver_kernel(
+    owners, shards, block, part_ref, send_ref, take_ref, out_ref,
+    parts, totals, leaving, arrived, placed, final, send_a, recv_a, send_b, recv_b, send_c, recv_c,
+):
+    chan, chans = partners("chan", owners)
+    time, times = partners("tm", shards)
+    per = part_ref.shape[1] // block
+    share = out_ref.shape[0]
+    wide = per * LAGS
+    greet([("tm", times[k]) for k in range(1, shards)] + [("chan", chans[k]) for k in range(1, owners)])
+
+    def by_source(k):
+        return remote(part_ref.at[times[k]], parts.at[k], send_a.at[k], recv_a.at[k], "tm", times[k])
+
+    def by_owner(k):
+        return remote(leaving.at[chans[k]], arrived.at[chan], send_b.at[k], recv_b.at[k], "chan", chans[k])
+
+    def by_row(k):
+        rows = pl.ds(pl.multiple_of(times[k] * share, share), share)
+        return remote(placed.at[rows, :], final.at[time], send_c.at[k], recv_c.at[k], "tm", times[k])
+
+    for k in range(1, shards):
+        by_source(k).start()
+    for k in range(1, shards):
+        by_source(k).wait()
+    for n in range(per):
+        rows = pl.ds(n * block, block)
+        total = part_ref[time, rows, :].astype(jnp.float32)
+        for k in range(1, shards):
+            total = total + parts[k, rows, :].astype(jnp.float32)
+        totals[:, pl.ds(n * LAGS, LAGS)] = total.astype(jnp.bfloat16)
+
+    for o in range(owners):
+        value = jnp.dot(send_ref[o], totals[...], preferred_element_type=jnp.float32)
+        leaving[o] = value.astype(jnp.bfloat16)
+    for k in range(1, owners):
+        by_owner(k).start()
+    arrived[chan] = leaving[chan]
+    for k in range(1, owners):
+        by_owner(k).wait()
+
+    if arrived.shape[1] % 16 == 0:
+        got = jnp.dot(
+            take_ref[...],
+            arrived[...].reshape(owners * arrived.shape[1], wide),
+            preferred_element_type=jnp.float32,
+        )
+    else:
+        slots = arrived.shape[1]
+        stacked = jnp.concatenate([arrived[o].astype(jnp.float32) for o in range(owners)], axis=0)
+        got = jnp.dot(
+            take_ref[...], stacked.astype(jnp.bfloat16), preferred_element_type=jnp.float32
+        )
+    placed[...] = got.astype(jnp.bfloat16)
+    for k in range(1, shards):
+        by_row(k).start()
+    final[time] = placed[pl.ds(pl.multiple_of(time * share, share), share), :]
+    for k in range(1, shards):
+        by_row(k).wait()
+    for m in range(shards):
+        out_ref[:, pl.ds(m * wide, wide)] = final[m].astype(jnp.float32)
+
+
+def deliver(partial, send, take, share):
+    shards, rows, lags = partial.shape
+    owners, slots, block = send.shape
+    wide = rows // block * lags
+    capacity = take.shape[0]
+    whole = pl.BlockSpec(memory_space=pltpu.VMEM)
+    bf16 = jnp.bfloat16
+    return pl.pallas_call(
+        functools.partial(deliver_kernel, owners, shards, block),
+        in_specs=[whole] * 3,
+        out_specs=whole,
+        out_shape=jax.ShapeDtypeStruct((share, shards * wide), jnp.float32),
+        scratch_shapes=[
+            pltpu.VMEM((shards, rows, lags), bf16),
+            pltpu.VMEM((block, wide), bf16),
+            pltpu.VMEM((owners, slots, wide), bf16),
+            pltpu.VMEM((owners, slots, wide), bf16),
+            pltpu.VMEM((capacity, wide), bf16),
+            pltpu.VMEM((shards, share, wide), bf16),
+        ]
+        + [pltpu.SemaphoreType.DMA((shards,))] * 2
+        + [pltpu.SemaphoreType.DMA((owners,))] * 2
+        + [pltpu.SemaphoreType.DMA((shards,))] * 2,
+        compiler_params=pltpu.CompilerParams(collective_id=1, has_side_effects=True),
+        name="deliver",
+    )(partial, send, take)
 
 
 def correlate_kernel(windows, sources, scale, own_ref, src_ref, inv_ref, o_ref, cross):
@@ -272,17 +452,9 @@
     sources = ids.shape[0]
     pick = (ids[:, None] == me * block + jnp.arange(block)[None, :]).astype(bf16)
     mine = jnp.dot(pick, traces, preferred_element_type=f32).astype(bf16)
-    source_rows = lax.psum(mine, "chan")
-
-    own = whiten(traces, tables)
-    src = whiten(source_rows, tables)
+    own, src = whiten(traces, mine, owners, windows, tables)
     partial = correlate(own, src, windows, scale, tables)
-
     per = sources // shards
-    parts = lax.all_to_all(
-        partial.reshape(shards, per, block, LAGS), "tm", split_axis=0, concat_axis=0, tiled=True
-    )
-    summed = jnp.sum(parts.astype(f32), axis=0).astype(bf16)
 
     source_block = jnp.floor_divide(owner_lists, block)
     matched = (owner_lists >= 0) & (source_block == me)
@@ -291,8 +463,6 @@
     chosen = matched[:, None, :] & (rank[:, None, :] == slot_ids[None, :, None])
     wanted = jnp.sum(jnp.where(chosen, owner_lists[:, None, :] - me * block + 1, 0), axis=2) - 1
     send = (wanted[:, :, None] == jnp.arange(block)[None, None, :]).astype(bf16)
-    outgoing = jnp.einsum("osc,ncl->onsl", send, summed, preferred_element_type=f32).astype(bf16)
-    arrived = lax.all_to_all(outgoing, "chan", split_axis=0, concat_axis=0, tiled=True)
 
     my_list = lax.dynamic_index_in_dim(owner_lists, me, 0, keepdims=False)
     my_block = jnp.floor_divide(my_list, block)
@@ -305,9 +475,10 @@
         & (my_block[:, None, None] == jnp.arange(owners)[None, :, None])
         & (earlier[:, None, None] == slot_ids[None, None, :])
     ).astype(bf16)
-    placed = jnp.einsum("rcs,cnsl->rnl", take, arrived, preferred_element_type=f32).astype(bf16)
-    result = lax.all_to_all(placed, "tm", split_axis=0, concat_axis=1, tiled=True)
-    return result.astype(f32)
+    result = deliver(
+        partial.reshape(shards, per * block, LAGS), send, take.reshape(capacity, owners * slots), share
+    )
+    return result.reshape(share, sources, LAGS)
 
 
 def solution(mesh):

time: 151 us -> 86.1 us (0.57)
  waiting for transfers between devices: 83 us -> 0 us
  Pallas kernels: 30.5 us -> 76.3 us
  between operations: 13.6 us -> 0.13 us
  blocking collectives: 8.39 us -> 0 us
  starting transfers between devices: 7.26 us -> 0 us
    psum x1 -> x0, waiting for transfers between devices: 66 us -> none  [body(): source_rows = lax.psum(mine, 'chan')]
    pallas_call x2, Pallas kernels: 13.5 us -> 59.3 us  [the longest x1 32.8 us: whiten(): pl.pallas_call(functools.partial(whiten_kernel, owners, windows), in_spec...]
    all_to_all x2 -> x0, waiting for transfers between devices: 17 us -> none  [the longest x1 8.54 us: body(): lax.all_to_all(partial.reshape(shards, per, block, LAGS), 'tm', split_axi...]
    all_to_all x1 -> x0, blocking collectives: 8.39 us -> none  [body(): lax.all_to_all(placed, 'tm', split_axis=0, concat_axis=1, tiled=True)]
    all_to_all x2 -> x0, starting transfers between devices: 7.25 us -> none  [the longest x1 3.78 us: body(): lax.all_to_all(outgoing, 'chan', split_axis=0, concat_axis=0, tiled=True)]
    unnamed x9 -> x10, local copies, waits for them, and re-layouts: 2.87 us -> 4.87 us
  transfers between devices with their start and end apart: 3 -> 0, of which waited for: 3 -> 0; matrix products, arithmetic and copies ran while one was open for 0% -> 0% of each run, Pallas kernels for 6% -> 0%
where the time goes in v2:
time: 86.1 us; the launch traced here: 85.5 us
  Pallas kernels  76.3 us (89%)
  local copies, waits for them, and re-layouts  6.31 us (7%)
  other arithmetic  1.52 us (2%)
  matrix products  1.26 us (1%)
    pallas_call x1, Pallas kernels, whiten(): pl.pallas_call(functools.partial(whiten_kernel, owners, windows), in_spec...  32.8 us
    pallas_call x1, Pallas kernels, deliver(): pl.pallas_call(functools.partial(deliver_kernel, owners, shards, block),...  26.5 us
    pallas_call x1, Pallas kernels, correlate(): pl.pallas_call(functools.partial(correlate_kernel, windows, sources, scal...  17 us
    unnamed x10, local copies, waits for them, and re-layouts  4.87 us

profile of v2, /device:TPU:0, one launch (start us, length us, event | category | flops | bytes accessed | tf_op | source)
XLA Modules:
  0.0 85.5 jit_solution(5521858828231191865)
XLA Ops:
  0.0 0.0 copy-start.3
  0.0 0.0 copy-start.2
  0.0 0.0 copy-start
  0.0 2.9 %copy.13 = bf16[8,8,4,4096]{3,1,2,0:T(8,128)(2,1)S(1)} copy(bf16[8,8,4,4096]{3,2,1,0:T(4,128)(2,1)} %bitcast.29) | data formatting | bytes 4194304
  2.9 0.0 copy-start.1
  2.9 0.0 copy-done.3
  2.9 0.0 copy-done.2
  2.9 0.1 fusion.14
  3.0 0.1 reshape.168
  3.1 0.0 copy-done
  3.1 0.6 gather_fusion
  3.7 1.3 %convolution_convert_fusion.mine_ref = bf16[16,16384]{1,0:T(8,128)(2,1)} fusion(bf16[64,16384]{1,0:T(8,128)(2,1)S(1)} %bitcast.26, s32[64]{0:T(128)S(1)} %iota_add_fusion, s32[16]{0:T(128)S(1)} %gather_fusion), kind=kOutput, calls=%fused_computation.1 | convolution fusion | flops 33817600 | bytes 2621760 | tf_op jit(solution)/shard_map/dot_general | solution.py:454
  5.0 0.0 copy-done.1
  5.0 32.8 %whiten.1 = (bf16[256,4096]{1,0:T(8,128)(2,1)}, bf16[64,4096]{1,0:T(8,128)(2,1)}) custom-call(bf16[64,16384]{1,0:T(8,128)(2,1)} %bitcast.27, bf16[16,16384]{1,0:T(8,128)(2,1)} %convolution_convert_fusion.mine_ref, f32[1,4096]{1,0:T(1,128)} %constant.65.clone.taper_ref, f32[9,256]{1,0:T(8,128)} %constant.66.clone.cos_ref, f32[9,256]{1,0:T(8,128)} %constant.67.clone.sin_ref, ...), custom_call_target="tpu_custom_call" | custom-call | tf_op jit(solution)/shard_map/whiten/pallas_call | solution.py:273
  37.8 17.0 %correlate.1 = bf16[1024,256]{1,0:T(8,128)(2,1)} custom-call(bf16[256,4096]{1,0:T(8,128)(2,1)} %get-tuple-element.7.own_ref, bf16[64,4096]{1,0:T(8,128)(2,1)} %get-tuple-element.8.src_ref, bf16[4096,256]{1,0:T(8,128)(2,1)} %constant.70.clone.inv_ref), custom_call_target="tpu_custom_call" | custom-call | tf_op jit(solution)/shard_map/correlate/pallas_call | solution.py:428
  54.8 0.3 reduce_window_sum.11
  55.1 0.2 select_reduce_fusion
  55.3 0.7 fusion.1.send_ref
  56.1 0.2 convert_reduce_fusion
  56.3 0.7 copy.12.take_ref
  57.0 26.5 %deliver.1 = f32[32,4096]{1,0:T(8,128)} custom-call(bf16[4,256,256]{2,1,0:T(8,128)(2,1)} %bitcast.28, bf16[8,16,64]{2,1,0:T(8,128)(2,1)} %fusion.1.send_ref, bf16[128,128]{1,0:T(8,128)(2,1)} %copy.12.take_ref), custom_call_target="tpu_custom_call" | custom-call | tf_op jit(solution)/shard_map/deliver/pallas_call | solution.py:364
  83.5 2.0 %copy.14 = f32[4,8,16,256]{3,2,1,0:T(8,128)} copy(f32[4,8,16,256]{3,1,2,0:T(8,128)} %bitcast.30) | data formatting | bytes 1048576
  (12 shorter events, 0.1 us)
Async XLA Ops:
  0.0 2.9 %copy-start.3 = (s32[2]{0:T(128)S(1)}, s32[2]{0:T(128)}, u32[]{:S(2)}) copy-start(s32[2]{0:T(128)} %param.12) | copy-start | bytes 28
  0.0 2.9 %copy-start.2 = (s32[2,8]{1,0:T(2,128)S(1)}, s32[2,8]{1,0:T(2,128)}, u32[]{:S(2)}) copy-start(s32[2,8]{1,0:T(2,128)} %param.13) | copy-start | bytes 196
  0.0 3.1 %copy-start = (s32[8,128]{1,0:T(8,128)S(1)}, s32[8,128]{1,0:T(8,128)}, u32[]{:S(2)}) copy-start(s32[8,128]{1,0:T(8,128)} %param.11) | copy-start | bytes 12292
  2.9 2.1 %copy-start.1 = (bf16[8,8,4,4096]{3,1,2,0:T(8,128)(2,1)}, bf16[8,8,4,4096]{3,1,2,0:T(8,128)(2,1)S(1)}, u32[]{:S(2)}) copy-start(bf16[8,8,4,4096]{3,1,2,0:T(8,128)(2,1)S(1)} %copy.13) | copy-start | bytes 6291460

commit v3 on v1

--- a/solution.py
+++ b/solution.py
@@ -94,8 +94,9 @@
     return out
 
 
-def whiten_kernel(x_ref, taper_ref, cos_ref, sin_ref, second_ref, count_ref, o_ref, turned, spec):
-    rows = x_ref.shape[0]
+def whiten_rows(load, store, tables, turned, spec):
+    taper_ref, cos_ref, sin_ref, second_ref, count_ref = tables
+    rows = turned.shape[0] // 9
     place = {q: (q - 1) * rows for q in range(1, 9)}
     place[0] = 8 * rows
     group = 16
@@ -107,7 +108,7 @@
             x = []
             for b in range(TB):
                 cols = pl.ds(b * TA + h * 128, 128)
-                v = x_ref[pl.ds(base, group), cols].astype(jnp.float32) * taper_ref[:, cols]
+                v = load(step, b * TA + h * 128).astype(jnp.float32) * taper_ref[:, cols]
                 x.append(v.astype(jnp.bfloat16).astype(jnp.float32))
             y = dft16_real(x)
             here = pl.ds(h * 128, 128)
@@ -171,88 +172,244 @@
                 suffix = suffix - mags[q]
                 inv = 1.0 / (smooth * count_ref[pl.ds(q, 1), :] + EPSILON)
                 done[half].append((part(q, 0) * inv, part(q, 1) * inv))
-        at = pl.ds(pl.multiple_of(step * 16, 16), 16)
         for q in range(TB):
             for p in range(2):
                 both = jnp.concatenate([done[0][q][p], done[1][q][p]], axis=0)
-                o_ref[at, pl.ds(q * 2 * KA + p * KA, KA)] = both.astype(jnp.bfloat16)
-
-
-def whiten(rows_by_window, tables):
-    rows = rows_by_window.shape[0]
-    windows = rows_by_window.shape[1] // L
-    taper, tcos, tsin, second, rcount, _ = tables
-    full = lambda v: pl.BlockSpec(v.shape, lambda w: (0, 0))
-    flops = 2 * 9 * rows * windows * 512 * 512
+                store(step, q * 2 * KA + p * KA, both.astype(jnp.bfloat16))
+
+
+def partners(axis, extent):
+    me = lax.axis_index(axis)
+    return me, [lax.rem(me + k, extent) for k in range(extent)]
+
+
+def remote(src, dst, send, recv, axis, device):
+    return pltpu.make_async_remote_copy(
+        src_ref=src,
+        dst_ref=dst,
+        send_sem=send,
+        recv_sem=recv,
+        device_id={axis: device},
+        device_id_type=pl.DeviceIdType.MESH,
+    )
+
+
+def greet(pairs):
+    barrier = pltpu.get_barrier_semaphore()
+    for axis, device in pairs:
+        pl.semaphore_signal(
+            barrier, inc=1, device_id={axis: device}, device_id_type=pl.DeviceIdType.MESH
+        )
+    pl.semaphore_wait(barrier, len(pairs))
+
+
+PIECES = 2
+
+
+def kernel(
+    owners, shards, block, windows, scale,
+    traces_ref, mine_ref, send_ref, take_ref, taper_ref, cos_ref, sin_ref, second_ref, count_ref, inv_hbm,
+    out_ref,
+    turned, spec, own, source, cross, inv_ref, shares, piece, gathered, part, parts, totals,
+    leaving, arrived, placed, final,
+    inv_sem, send_r, recv_r, send_g, recv_g, send_a, recv_a, send_b, recv_b, send_c, recv_c,
+):
+    tables = (taper_ref, cos_ref, sin_ref, second_ref, count_ref)
+    f32, bf16 = jnp.float32, jnp.bfloat16
+    chunks, group, _ = mine_ref.shape
+    held = group // windows
+    width = L // owners
+    per = part.shape[1] // block
+    ends = held // per
+    share = out_ref.shape[0]
+    wide = totals.shape[2]
+    chan, chans = partners("chan", owners)
+    time, times = partners("tm", shards)
+    home = time // ends
+    greet([("chan", chans[k]) for k in range(1, owners)] + [("tm", times[k]) for k in range(1, shards)])
+
+    def cut(device):
+        return pl.ds(pl.multiple_of(device * width, 128), width)
+
+    def chunk_of(s):
+        return lax.rem(home + 1 + s, chunks)
+
+    def reduce_copy(s, k):
+        src = mine_ref.at[chunk_of(s), :, cut(chans[k])]
+        return remote(src, shares.at[s, k], send_r.at[s, k], recv_r.at[s, k], "chan", chans[k])
+
+    def gather_copy(s, k):
+        dst = gathered.at[s, :, cut(chan)]
+        return remote(piece.at[s], dst, send_g.at[s, k], recv_g.at[s, k], "chan", chans[k])
+
+    for s in range(chunks):
+        for k in range(1, owners):
+            reduce_copy(s, k).start()
+    inv_copy = pltpu.make_async_copy(inv_hbm, inv_ref, inv_sem)
+    inv_copy.start()
+
+    @pl.loop(0, windows)
+    def _(w):
+        def load(step, col):
+            at = pl.ds(pl.multiple_of(w * block + step * group, group), group)
+            return traces_ref[at, pl.ds(col, 128)]
+
+        def store(step, col, value):
+            at = pl.ds(pl.multiple_of(w * block + step * group, group), group)
+            own[at, pl.ds(col, KA)] = value.astype(f32)
+
+        whiten_rows(load, store, tables, turned, spec)
+
+        total = mine_ref[chunk_of(w), :, cut(chan)].astype(f32)
+        for k in range(1, owners):
+            reduce_copy(w, k).wait()
+            total = total + shares[w, k].astype(f32)
+        piece[w] = total.astype(bf16)
+        gathered[w, :, cut(chan)] = total.astype(bf16)
+        for k in range(1, owners):
+            gather_copy(w, k).start()
+
+    inv_copy.wait()
+
+    @pl.loop(0, chunks)
+    def _(s):
+        for k in range(1, owners):
+            gather_copy(s, k).wait()
+
+        def load(step, col):
+            return gathered[s, :, pl.ds(col, 128)]
+
+        def store(step, col, value):
+            source[:, pl.ds(col, KA)] = value.astype(f32)
+
+        whiten_rows(load, store, tables, turned.at[0 : 9 * group, :], spec.at[0 : 9 * group, :])
+
+        @pl.loop(0, TB)
+        def _(q):
+            col_re = pl.ds(pl.multiple_of(q * 2 * KA, KA), KA)
+            col_im = pl.ds(pl.multiple_of(q * 2 * KA + KA, KA), KA)
+            rows = [[pl.ds(w * held + n, 1) for w in range(windows)] for n in range(held)]
+            wave = [[(source[r, col_re], source[r, col_im]) for r in line] for line in rows]
+            wave = [
+                [tuple(jnp.broadcast_to(v, (16, KA)) for v in (x, y, x - y)) for x, y in line]
+                for line in wave
+            ]
+            for g in range(block // 16):
+                at = [pl.ds(w * block + g * 16, 16) for w in range(windows)]
+                a = [own[r, col_re] for r in at]
+                b = [own[r, col_im] for r in at]
+                c = [x + y for x, y in zip(a, b)]
+                for n in range(held):
+                    sums = []
+                    for factor, which in ((a, 0), (b, 1), (c, 2)):
+                        total = factor[0] * wave[n][0][which]
+                        for w in range(1, windows):
+                            total = total + factor[w] * wave[n][w][which]
+                        sums.append(total)
+                    to = pl.ds(n * block + g * 16, 16)
+                    cross[to, col_re] = (sums[0] + sums[1]).astype(bf16)
+                    cross[to, col_im] = (sums[2] - sums[0] + sums[1]).astype(bf16)
+
+        out = jnp.dot(cross[...], inv_ref[...], preferred_element_type=f32) * scale
+        out = out.astype(bf16)
+        for j in range(ends):
+            end = chunk_of(s) * ends + j
+            part[end] = out[j * per * block : (j + 1) * per * block]
+            k = lax.rem(end - time + shards, shards)
+
+            @pl.when(k != 0)
+            def _():
+                remote(part.at[end], parts.at[k], send_a.at[k], recv_a.at[k], "tm", end).start()
+
+    def by_source(k):
+        return remote(part.at[times[k]], parts.at[k], send_a.at[k], recv_a.at[k], "tm", times[k])
+
+    def by_owner(p, k):
+        src, dst = leaving.at[p, chans[k]], arrived.at[p, chan]
+        return remote(src, dst, send_b.at[p, k], recv_b.at[p, k], "chan", chans[k])
+
+    def by_row(p, k):
+        rows = pl.ds(pl.multiple_of(times[k] * share, share), share)
+        src, dst = placed.at[p, rows, :], final.at[p, time]
+        return remote(src, dst, send_c.at[p, k], recv_c.at[p, k], "tm", times[k])
+
+    for k in range(1, shards):
+        by_source(k).wait()
+    each = per // PIECES
+    for p in range(PIECES):
+        for n in range(each):
+            rows = pl.ds((p * each + n) * block, block)
+            total = part[time, rows, :].astype(f32)
+            for k in range(1, shards):
+                total = total + parts[k, rows, :].astype(f32)
+            totals[p, :, pl.ds(n * LAGS, LAGS)] = total.astype(bf16)
+        for o in range(owners):
+            leaving[p, o] = jnp.dot(send_ref[o], totals[p], preferred_element_type=f32).astype(bf16)
+        for k in range(1, owners):
+            by_owner(p, k).start()
+        arrived[p, chan] = leaving[p, chan]
+
+    slots = arrived.shape[2]
+    for p in range(PIECES):
+        for k in range(1, owners):
+            by_owner(p, k).wait()
+        if slots % 16 == 0:
+            stacked = arrived[p].reshape(owners * slots, wide)
+        else:
+            stacked = jnp.concatenate([arrived[p, o].astype(f32) for o in range(owners)], axis=0).astype(bf16)
+        placed[p] = jnp.dot(take_ref[...], stacked, preferred_element_type=f32).astype(bf16)
+        for k in range(1, shards):
+            by_row(p, k).start()
+        final[p, time] = placed[p, pl.ds(pl.multiple_of(time * share, share), share), :]
+    for p in range(PIECES):
+        for k in range(1, shards):
+            by_row(p, k).wait()
+        for m in range(shards):
+            out_ref[:, pl.ds((m * PIECES + p) * wide, wide)] = final[p, m].astype(f32)
+
+
+def run(traces, mine, send, take, shards, share, scale, tables):
+    chunks, group, _ = mine.shape
+    owners, slots, block = send.shape
+    windows = traces.shape[0] // block
+    held = group // windows
+    sources = chunks * held
+    per = sources // shards
+    wide = per // PIECES * LAGS
+    capacity = take.shape[0]
+    most = max(block, group)
+    vmem = pl.BlockSpec(memory_space=pltpu.VMEM)
+    bf16, f32 = jnp.bfloat16, jnp.float32
+    sems = lambda *shape: [pltpu.SemaphoreType.DMA(shape)] * 2
     return pl.pallas_call(
-        whiten_kernel,
-        grid=(windows,),
-        in_specs=[pl.BlockSpec((rows, L), lambda w: (0, w))]
-        + [full(v) for v in (taper, tcos, tsin, second, rcount)],
-        out_specs=pl.BlockSpec((rows, L), lambda w: (w, 0)),
-        out_shape=jax.ShapeDtypeStruct((windows * rows, L), jnp.bfloat16),
+        functools.partial(kernel, owners, shards, block, windows, scale),
+        in_specs=[vmem] * 9 + [pl.BlockSpec(memory_space=pl.ANY)],
+        out_specs=vmem,
+        out_shape=jax.ShapeDtypeStruct((share, sources * LAGS), f32),
         scratch_shapes=[
-            pltpu.VMEM((9 * rows, 2 * TA), jnp.bfloat16),
-            pltpu.VMEM((9 * rows, 4 * KA), jnp.float32),
-        ],
-        cost_estimate=pl.CostEstimate(
-            flops=flops, bytes_accessed=4 * rows * windows * L, transcendentals=0
-        ),
-        name="whiten",
-    )(rows_by_window, taper, tcos, tsin, second, rcount)
-
-
-def correlate_kernel(windows, sources, scale, own_ref, src_ref, inv_ref, o_ref, cross):
-    chans = own_ref.shape[0] // windows
-
-    @pl.loop(0, TB)
-    def _(q):
-        col_re = pl.ds(pl.multiple_of(q * 2 * KA, KA), KA)
-        col_im = pl.ds(pl.multiple_of(q * 2 * KA + KA, KA), KA)
-        for n in range(sources):
-            s_re = [
-                jnp.broadcast_to(src_ref[pl.ds(w * sources + n, 1), col_re], (16, KA)).astype(jnp.float32)
-                for w in range(windows)
-            ]
-            s_im = [
-                jnp.broadcast_to(src_ref[pl.ds(w * sources + n, 1), col_im], (16, KA)).astype(jnp.float32)
-                for w in range(windows)
-            ]
-            for g in range(chans // 16):
-                re = im = None
-                for w in range(windows):
-                    at = pl.ds(w * chans + g * 16, 16)
-                    a = own_ref[at, col_re].astype(jnp.float32)
-                    b = own_ref[at, col_im].astype(jnp.float32)
-                    r = a * s_re[w] + b * s_im[w]
-                    i = b * s_re[w] - a * s_im[w]
-                    re = r if re is None else re + r
-                    im = i if im is None else im + i
-                at = pl.ds(n * chans + g * 16, 16)
-                cross[at, col_re] = re.astype(jnp.bfloat16)
-                cross[at, col_im] = im.astype(jnp.bfloat16)
-
-    tile = math.gcd(sources * chans, 256)
-
-    @pl.loop(0, sources * chans // tile)
-    def _(step):
-        at = pl.ds(pl.multiple_of(step * tile, tile), tile)
-        out = jnp.dot(cross[at, :], inv_ref[...], preferred_element_type=jnp.float32)
-        o_ref[at, :] = (out * scale).astype(jnp.bfloat16)
-
-
-def correlate(own, src, windows, scale, tables):
-    chans, sources = own.shape[0] // windows, src.shape[0] // windows
-    inverse = tables[5]
-    whole = pl.BlockSpec(memory_space=pltpu.VMEM)
-    return pl.pallas_call(
-        functools.partial(correlate_kernel, windows, sources, scale),
-        in_specs=[whole] * 3,
-        out_specs=whole,
-        out_shape=jax.ShapeDtypeStruct((sources * chans, LAGS), jnp.bfloat16),
-        scratch_shapes=[pltpu.VMEM((sources * chans, L), jnp.bfloat16)],
-        name="correlate",
-    )(own, src, inverse)
+            pltpu.VMEM((9 * most, 2 * TA), bf16),
+            pltpu.VMEM((9 * most, 4 * KA), f32),
+            pltpu.VMEM((windows * block, L), f32),
+            pltpu.VMEM((group, L), f32),
+            pltpu.VMEM((held * block, L), bf16),
+            pltpu.VMEM((L, LAGS), bf16),
+            pltpu.VMEM((chunks, owners, group, L // owners), bf16),
+            pltpu.VMEM((chunks, group, L // owners), bf16),
+            pltpu.VMEM((chunks, group, L), bf16),
+            pltpu.VMEM((shards, per * block, LAGS), bf16),
+            pltpu.VMEM((shards, per * block, LAGS), bf16),
+            pltpu.VMEM((PIECES, block, wide), bf16),
+            pltpu.VMEM((PIECES, owners, slots, wide), bf16),
+            pltpu.VMEM((PIECES, owners, slots, wide), bf16),
+            pltpu.VMEM((PIECES, capacity, wide), bf16),
+            pltpu.VMEM((PIECES, shards, share, wide), bf16),
+            pltpu.SemaphoreType.DMA,
+        ]
+        + sems(chunks, owners) + sems(chunks, owners)
+        + sems(shards) + sems(PIECES, owners) + sems(PIECES, shards),
+        compiler_params=pltpu.CompilerParams(collective_id=0, has_side_effects=True),
+        name="correlations",
+    )(traces, mine, send, take, *tables)
 
 
 def body(raw_traces, owner_lists, source_owner, source_slot):
@@ -267,22 +424,18 @@
     scale = 1.0 / math.sqrt(windows * shards * HALF)
     bf16, f32 = jnp.bfloat16, jnp.float32
 
-    traces = raw_traces.reshape(block, windows * length)
+    held = 16 // windows
     ids = owner_lists[source_owner[:, None], source_slot].reshape(-1)
     sources = ids.shape[0]
-    pick = (ids[:, None] == me * block + jnp.arange(block)[None, :]).astype(bf16)
+    chunks = sources // held
+    assert chunks == windows and held % (sources // shards) == 0
+    traces = jnp.transpose(raw_traces, (1, 0, 2)).reshape(windows * block, length)
+    channel = jnp.broadcast_to(ids.reshape(chunks, 1, held) - me * block, (chunks, windows, held))
+    inside = (channel >= 0) & (channel < block)
+    row = jnp.where(inside, channel + block * jnp.arange(windows, dtype=jnp.int32)[None, :, None], -1)
+    pick = (row.reshape(-1)[:, None] == jnp.arange(windows * block, dtype=jnp.int32)[None, :]).astype(bf16)
     mine = jnp.dot(pick, traces, preferred_element_type=f32).astype(bf16)
-    source_rows = lax.psum(mine, "chan")
-
-    own = whiten(traces, tables)
-    src = whiten(source_rows, tables)
-    partial = correlate(own, src, windows, scale, tables)
-
-    per = sources // shards
-    parts = lax.all_to_all(
-        partial.reshape(shards, per, block, LAGS), "tm", split_axis=0, concat_axis=0, tiled=True
-    )
-    summed = jnp.sum(parts.astype(f32), axis=0).astype(bf16)
+    mine = mine.reshape(chunks, windows * held, length)
 
     source_block = jnp.floor_divide(owner_lists, block)
     matched = (owner_lists >= 0) & (source_block == me)
@@ -291,8 +444,6 @@
     chosen = matched[:, None, :] & (rank[:, None, :] == slot_ids[None, :, None])
     wanted = jnp.sum(jnp.where(chosen, owner_lists[:, None, :] - me * block + 1, 0), axis=2) - 1
     send = (wanted[:, :, None] == jnp.arange(block)[None, None, :]).astype(bf16)
-    outgoing = jnp.einsum("osc,ncl->onsl", send, summed, preferred_element_type=f32).astype(bf16)
-    arrived = lax.all_to_all(outgoing, "chan", split_axis=0, concat_axis=0, tiled=True)
 
     my_list = lax.dynamic_index_in_dim(owner_lists, me, 0, keepdims=False)
     my_block = jnp.floor_divide(my_list, block)
@@ -305,9 +456,10 @@
         & (my_block[:, None, None] == jnp.arange(owners)[None, :, None])
         & (earlier[:, None, None] == slot_ids[None, None, :])
     ).astype(bf16)
-    placed = jnp.einsum("rcs,cnsl->rnl", take, arrived, preferred_element_type=f32).astype(bf16)
-    result = lax.all_to_all(placed, "tm", split_axis=0, concat_axis=1, tiled=True)
-    return result.astype(f32)
+    result = run(
+        traces, mine, send, take.reshape(capacity, owners * slots), shards, share, scale, tables
+    )
+    return result.reshape(share, sources, LAGS)
 
 
 def solution(mesh):

time: 151 us -> 70.3 us (0.47)
  waiting for transfers between devices: 83 us -> 0 us
  Pallas kernels: 30.5 us -> 56.3 us
  between operations: 13.6 us -> 0.08 us
  blocking collectives: 8.39 us -> 0 us
  starting transfers between devices: 7.26 us -> 0 us
  other arithmetic: 0.97 us -> 5.01 us
  local copies, waits for them, and re-layouts: 5.56 us -> 7.07 us
    psum x1 -> x0, waiting for transfers between devices: 66 us -> none  [body(): source_rows = lax.psum(mine, 'chan')]
    pallas_call x3 -> x1, Pallas kernels: 30.5 us -> 56.3 us  [run(): pl.pallas_call(functools.partial(kernel, owners, shards, block, windows,...]
    all_to_all x2 -> x0, waiting for transfers between devices: 17 us -> none  [the longest x1 8.54 us: body(): lax.all_to_all(partial.reshape(shards, per, block, LAGS), 'tm', split_axi...]
    all_to_all x1 -> x0, blocking collectives: 8.39 us -> none  [body(): lax.all_to_all(placed, 'tm', split_axis=0, concat_axis=1, tiled=True)]
    all_to_all x2 -> x0, starting transfers between devices: 7.25 us -> none  [the longest x1 3.78 us: body(): lax.all_to_all(outgoing, 'chan', split_axis=0, concat_axis=0, tiled=True)]
    transpose x0 -> x1, local copies, waits for them, and re-layouts: none -> 2.74 us  [body(): jnp.transpose(raw_traces, (1, 0, 2)).reshape(windows * block, length)]
  transfers between devices with their start and end apart: 3 -> 0, of which waited for: 3 -> 0; matrix products, arithmetic and copies ran while one was open for 0% -> 0% of each run, Pallas kernels for 6% -> 0%
where the time goes in v3:
time: 70.3 us; the launch traced here: 70 us
  Pallas kernels  56.3 us (80%)
  local copies, waits for them, and re-layouts  7.07 us (10%)
  other arithmetic  5.01 us (7%)
  matrix products  1.47 us (2%)
    pallas_call x1, Pallas kernels, run(): pl.pallas_call(functools.partial(kernel, owners, shards, block, windows,...  56.3 us
    transpose x1, local copies, waits for them, and re-layouts, body(): jnp.transpose(raw_traces, (1, 0, 2)).reshape(windows * block, length)  2.74 us
    unnamed x3, local copies, waits for them, and re-layouts  2 us
    dot_general x1, matrix products, body(): mine = jnp.dot(pick, traces, preferred_element_type=f32).astype(bf16)  1.47 us
    concatenate x2, other arithmetic, body(): ids = owner_lists[source_owner[:, None], source_slot].reshape(-1)  1.41 us

profile of v3, /device:TPU:0, one launch (start us, length us, event | category | flops | bytes accessed | tf_op | source)
XLA Modules:
  0.0 70.0 jit_solution(9266250425972799289)
XLA Ops:
  0.0 0.7 fusion.14
  0.7 0.7 %fusion.12 = s32[2,8,1]{1,0,2:T(2,128)S(1)} fusion(s32[2,8]{1,0:T(2,128)} %param.13, s32[2]{0:T(128)S(1)} %fusion.14), kind=kLoop, calls=%fused_computation.45 | loop fusion | flops 96 | bytes 136 | tf_op jit(solution)/shard_map/concatenate | solution.py:428
  1.4 0.1 reshape.207
  1.5 1.4 %gather_fusion = s32[16]{0:T(128)S(1)} fusion(s32[8,128]{1,0:T(8,128)} %param.11, s32[16]{0:T(128)S(1)} %reshape.207), kind=kCustom, calls=%fused_computation | custom fusion | bytes 256 | tf_op jit(solution)/shard_map/gather | solution.py:428
  2.9 0.7 %bitcast_compare_fusion = (pred[128]{0:T(512)(128)(4,1)S(1)}, s32[1,128]{1,0:T(1,128)S(1)}) fusion(s32[8,128]{1,0:T(8,128)} %param.11, s32[]{:T(128)S(6)} %select_n.53), kind=kLoop, calls=%fused_computation.49 | loop fusion | flops 128 | bytes 1156 | tf_op jit(solution)/shard_map/ge | solution.py:450
  3.6 0.2 convert_reduce_fusion
  3.8 0.1 sub.45
  3.9 0.7 %fusion.16 = (s32[8,128]{1,0:T(8,128)S(1)}, pred[8,128]{1,0:T(8,128)(4,1)S(1)}) fusion(s32[]{:T(128)S(6)} %axis_index.15, s32[8,128]{1,0:T(8,128)} %param.11), kind=kLoop, calls=%fused_computation.54 | loop fusion | flops 19456 | bytes 9220 | tf_op jit(solution)/shard_map/convert_element_type | solution.py:442
  4.6 0.3 reduce_window_sum.11
  4.9 0.7 subtract_add_fusion
  5.6 0.2 select_reduce_fusion
  5.8 0.1 add_select_fusion
  5.9 0.1 select_n.50
  6.0 0.7 fusion.1.send_ref
  6.7 0.7 %copy.15.take_ref = bf16[128,128]{1,0:T(8,128)(2,1)} copy(bf16[128,128]{0,1:T(8,128)(2,1)S(1)} %bitcast.31) | data formatting | bytes 65536 | tf_op jit(solution)/shard_map/convert_element_type | solution.py:458
  7.4 2.7 %copy.14 = bf16[4,64,4096]{2,1,0:T(8,128)(2,1)S(1)} copy(bf16[4,64,4096]{2,0,1:T(4,128)(2,1)} %bitcast.29) | data formatting | bytes 4194304 | tf_op jit(solution)/shard_map/transpose | solution.py:432
  10.1 0.0 copy-start
  10.1 1.5 %convolution_convert_fusion = bf16[64,4096]{1,0:T(8,128)(2,1)} fusion(bf16[256,4096]{1,0:T(8,128)(2,1)S(1)} %bitcast.26, s32[64]{0:T(128)S(1)} %select_n.50), kind=kOutput, calls=%fused_computation.1 | convolution fusion | flops 134496256 | bytes 2621696 | tf_op jit(solution)/shard_map/dot_general | solution.py:437
  11.6 0.0 copy-done
  11.6 56.3 %correlations.1 = f32[32,4096]{1,0:T(8,128)} custom-call(bf16[256,4096]{1,0:T(8,128)(2,1)} %bitcast.27, bf16[4,16,4096]{2,1,0:T(8,128)(2,1)} %bitcast.30, bf16[8,16,64]{2,1,0:T(8,128)(2,1)} %fusion.1.send_ref, bf16[128,128]{1,0:T(8,128)(2,1)} %copy.15.take_ref, f32[1,4096]{1,0:T(1,128)} %constant.69.clone.taper_ref, f32[9,256]{1,0:T(8,128)} %constant.70.clone.cos_ref, ...), custom_call_target="tpu_custom_call" | custom-call | tf_op jit(solution)/shard_map/correlations/pallas_call | solution.py:384
  68.0 2.0 %copy.16 = f32[4,8,16,256]{3,2,1,0:T(8,128)} copy(f32[4,8,16,256]{3,1,2,0:T(8,128)} %bitcast.28) | data formatting | bytes 1048576
  (10 shorter events, 0.1 us)
Async XLA Ops:
  10.1 1.5 %copy-start = (bf16[4,64,4096]{2,1,0:T(8,128)(2,1)}, bf16[4,64,4096]{2,1,0:T(8,128)(2,1)S(1)}, u32[]{:S(2)}) copy-start(bf16[4,64,4096]{2,1,0:T(8,128)(2,1)S(1)} %copy.14) | copy-start | bytes 6291460

commit v4 on v3

--- a/solution.py
+++ b/solution.py
@@ -200,7 +200,7 @@
         pl.semaphore_signal(
             barrier, inc=1, device_id={axis: device}, device_id_type=pl.DeviceIdType.MESH
         )
-    pl.semaphore_wait(barrier, len(pairs))
+    return lambda: pl.semaphore_wait(barrier, len(pairs))
 
 
 PIECES = 2
@@ -208,9 +208,9 @@
 
 def kernel(
     owners, shards, block, windows, scale,
-    traces_ref, mine_ref, send_ref, take_ref, taper_ref, cos_ref, sin_ref, second_ref, count_ref, inv_hbm,
+    slots, traces_ref, lists_ref, lists_s, owner_s, slot_s, taper_ref, cos_ref, sin_ref, second_ref, count_ref, inv_hbm,
     out_ref,
-    turned, spec, own, source, cross, inv_ref, shares, piece, gathered, part, parts, totals,
+    mine_ref, send_ref, take_ref, turned, spec, own, source, cross, inv_ref, shares, piece, gathered, part, parts, totals,
     leaving, arrived, placed, final,
     inv_sem, send_r, recv_r, send_g, recv_g, send_a, recv_a, send_b, recv_b, send_c, recv_c,
 ):
@@ -226,7 +226,31 @@
     chan, chans = partners("chan", owners)
     time, times = partners("tm", shards)
     home = time // ends
-    greet([("chan", chans[k]) for k in range(1, owners)] + [("tm", times[k]) for k in range(1, shards)])
+    pairs = [("chan", chans[k]) for k in range(1, owners)] + [("tm", times[k]) for k in range(1, shards)]
+    all_here = greet(pairs)
+
+    def iota(shape, dim):
+        return lax.broadcasted_iota(jnp.int32, shape, dim)
+
+    shape = (chunks * group, windows * block)
+    row, col = iota(shape, 0), iota(shape, 1)
+    which = row // group * held + row % held
+    wanted = jnp.full(shape, -1, jnp.int32)
+    steps, each_step = slot_s.shape
+    for i in range(steps * each_step):
+        channel = lists_s[owner_s[i // each_step], slot_s[i // each_step, i % each_step]]
+        wanted = jnp.where(which == i, channel, wanted)
+    hit = (wanted == chan * block + col % block) & (col // block == row // held % windows)
+    pick = jnp.where(hit, 1.0, 0.0).astype(bf16)
+
+    @pl.loop(0, L // 1024)
+    def _(t):
+        at = pl.ds(pl.multiple_of(t * 1024, 1024), 1024)
+        rows = jnp.dot(pick, traces_ref[:, at], preferred_element_type=f32).astype(bf16)
+        for g in range(chunks):
+            mine_ref[g, :, at] = rows[g * group : (g + 1) * group]
+
+    all_here()
 
     def cut(device):
         return pl.ds(pl.multiple_of(device * width, 128), width)
@@ -242,11 +266,35 @@
         dst = gathered.at[s, :, cut(chan)]
         return remote(piece.at[s], dst, send_g.at[s, k], recv_g.at[s, k], "chan", chans[k])
 
-    for s in range(chunks):
+    for s in range(2):
         for k in range(1, owners):
             reduce_copy(s, k).start()
     inv_copy = pltpu.make_async_copy(inv_hbm, inv_ref, inv_sem)
     inv_copy.start()
+
+    capacity = lists_ref.shape[1]
+    before = jnp.where(iota((capacity, capacity), 0) <= iota((capacity, capacity), 1), 1.0, 0.0)
+    lists = lists_ref[...]
+    here = (lists >= chan * block) & (lists < (chan + 1) * block)
+    inside = jnp.where(here, lists - chan * block, -1).astype(f32)
+    wall = (owners * slots, capacity)
+    spread = jnp.where(
+        iota((owners * slots, owners), 0) // slots == iota((owners * slots, owners), 1), 1.0, 0.0
+    )
+    offset = jnp.dot(spread, inside, preferred_element_type=f32)
+    live = offset >= 0
+    slot = (iota(wall, 0) % slots + 1).astype(f32)
+    rank = jnp.dot(jnp.where(live, 1.0, 0.0), before, preferred_element_type=f32)
+    channel = jnp.sum(jnp.where(live & (rank == slot), offset + 1.0, 0.0), axis=1, keepdims=True) - 1.0
+    send_ref[...] = jnp.where(
+        channel == iota((owners * slots, block), 1).astype(f32), 1.0, 0.0
+    )
+    listed = jnp.broadcast_to(lists_ref[pl.ds(chan, 1), :], wall)
+    start = iota(wall, 0) // slots * block
+    found = (listed >= start) & (listed < start + block)
+    rank = jnp.dot(jnp.where(found, 1.0, 0.0), before, preferred_element_type=f32)
+    take = jnp.where(found & (rank == slot), 1.0, 0.0)
+    take_ref[...] = take.T.astype(bf16)
 
     @pl.loop(0, windows)
     def _(w):
@@ -268,6 +316,11 @@
         gathered[w, :, cut(chan)] = total.astype(bf16)
         for k in range(1, owners):
             gather_copy(w, k).start()
+
+        @pl.when(w + 2 < chunks)
+        def _():
+            for k in range(1, owners):
+                reduce_copy(w + 2, k).start()
 
     inv_copy.wait()
 
@@ -343,13 +396,17 @@
             for k in range(1, shards):
                 total = total + parts[k, rows, :].astype(f32)
             totals[p, :, pl.ds(n * LAGS, LAGS)] = total.astype(bf16)
-        for o in range(owners):
-            leaving[p, o] = jnp.dot(send_ref[o], totals[p], preferred_element_type=f32).astype(bf16)
+        if slots % 16 == 0:
+            value = jnp.dot(send_ref[...].astype(bf16), totals[p], preferred_element_type=f32)
+            leaving[p] = value.astype(bf16).reshape(owners, slots, wide)
+        else:
+            for o in range(owners):
+                mask = send_ref[pl.ds(o * slots, slots), :].astype(bf16)
+                leaving[p, o] = jnp.dot(mask, totals[p], preferred_element_type=f32).astype(bf16)
         for k in range(1, owners):
             by_owner(p, k).start()
         arrived[p, chan] = leaving[p, chan]
 
-    slots = arrived.shape[2]
     for p in range(PIECES):
         for k in range(1, owners):
             by_owner(p, k).wait()
@@ -365,28 +422,37 @@
         for k in range(1, shards):
             by_row(p, k).wait()
         for m in range(shards):
-            out_ref[:, pl.ds((m * PIECES + p) * wide, wide)] = final[p, m].astype(f32)
-
-
-def run(traces, mine, send, take, shards, share, scale, tables):
-    chunks, group, _ = mine.shape
-    owners, slots, block = send.shape
-    windows = traces.shape[0] // block
+            for n in range(each):
+                value = final[p, m, :, pl.ds(n * LAGS, LAGS)].astype(f32)
+                out_ref[:, m * per + p * each + n, :] = value
+
+
+def run(traces, lists, source_owner, source_slot, shards, owners, windows, scale, tables):
+    capacity = lists.shape[1]
+    block = traces.shape[0] // windows
+    group = 16
     held = group // windows
-    sources = chunks * held
+    sources = source_slot.size
+    chunks = sources // held
+    assert chunks == windows and held % (sources // shards) == 0
+    slots = (capacity + owners - 1) // owners
+    share = capacity // shards
+    smem = pl.BlockSpec(memory_space=pltpu.SMEM)
     per = sources // shards
     wide = per // PIECES * LAGS
-    capacity = take.shape[0]
     most = max(block, group)
     vmem = pl.BlockSpec(memory_space=pltpu.VMEM)
     bf16, f32 = jnp.bfloat16, jnp.float32
     sems = lambda *shape: [pltpu.SemaphoreType.DMA(shape)] * 2
     return pl.pallas_call(
-        functools.partial(kernel, owners, shards, block, windows, scale),
-        in_specs=[vmem] * 9 + [pl.BlockSpec(memory_space=pl.ANY)],
+        functools.partial(kernel, owners, shards, block, windows, scale, slots),
+        in_specs=[vmem] * 2 + [smem] * 3 + [vmem] * 5 + [pl.BlockSpec(memory_space=pl.ANY)],
         out_specs=vmem,
-        out_shape=jax.ShapeDtypeStruct((share, sources * LAGS), f32),
+        out_shape=jax.ShapeDtypeStruct((share, sources, LAGS), f32),
         scratch_shapes=[
+            pltpu.VMEM((chunks, group, L), bf16),
+            pltpu.VMEM((owners * slots, block), f32),
+            pltpu.VMEM((capacity, owners * slots), bf16),
             pltpu.VMEM((9 * most, 2 * TA), bf16),
             pltpu.VMEM((9 * most, 4 * KA), f32),
             pltpu.VMEM((windows * block, L), f32),
@@ -409,57 +475,18 @@
         + sems(shards) + sems(PIECES, owners) + sems(PIECES, shards),
         compiler_params=pltpu.CompilerParams(collective_id=0, has_side_effects=True),
         name="correlations",
-    )(traces, mine, send, take, *tables)
+    )(traces, lists, lists, source_owner, source_slot, *tables)
 
 
 def body(raw_traces, owner_lists, source_owner, source_slot):
     block, windows, length = raw_traces.shape
-    owners = lax.axis_size("chan")
-    shards = lax.axis_size("tm")
-    capacity = owner_lists.shape[1]
-    slots = (capacity + owners - 1) // owners
-    share = capacity // shards
-    me = lax.axis_index("chan")
+    owners, shards = lax.axis_size("chan"), lax.axis_size("tm")
     tables = tuple(jnp.asarray(t) for t in make_tables())
     scale = 1.0 / math.sqrt(windows * shards * HALF)
-    bf16, f32 = jnp.bfloat16, jnp.float32
-
-    held = 16 // windows
-    ids = owner_lists[source_owner[:, None], source_slot].reshape(-1)
-    sources = ids.shape[0]
-    chunks = sources // held
-    assert chunks == windows and held % (sources // shards) == 0
     traces = jnp.transpose(raw_traces, (1, 0, 2)).reshape(windows * block, length)
-    channel = jnp.broadcast_to(ids.reshape(chunks, 1, held) - me * block, (chunks, windows, held))
-    inside = (channel >= 0) & (channel < block)
-    row = jnp.where(inside, channel + block * jnp.arange(windows, dtype=jnp.int32)[None, :, None], -1)
-    pick = (row.reshape(-1)[:, None] == jnp.arange(windows * block, dtype=jnp.int32)[None, :]).astype(bf16)
-    mine = jnp.dot(pick, traces, preferred_element_type=f32).astype(bf16)
-    mine = mine.reshape(chunks, windows * held, length)
-
-    source_block = jnp.floor_divide(owner_lists, block)
-    matched = (owner_lists >= 0) & (source_block == me)
-    rank = jnp.cumsum(matched.astype(jnp.int32), axis=1) - 1
-    slot_ids = jnp.arange(slots, dtype=jnp.int32)
-    chosen = matched[:, None, :] & (rank[:, None, :] == slot_ids[None, :, None])
-    wanted = jnp.sum(jnp.where(chosen, owner_lists[:, None, :] - me * block + 1, 0), axis=2) - 1
-    send = (wanted[:, :, None] == jnp.arange(block)[None, None, :]).astype(bf16)
-
-    my_list = lax.dynamic_index_in_dim(owner_lists, me, 0, keepdims=False)
-    my_block = jnp.floor_divide(my_list, block)
-    live = my_list >= 0
-    position = jnp.arange(capacity, dtype=jnp.int32)
-    same = (my_block[:, None] == my_block[None, :]) & (position[None, :] < position[:, None]) & live[None, :]
-    earlier = jnp.sum(same.astype(jnp.int32), axis=1)
-    take = (
-        live[:, None, None]
-        & (my_block[:, None, None] == jnp.arange(owners)[None, :, None])
-        & (earlier[:, None, None] == slot_ids[None, None, :])
-    ).astype(bf16)
-    result = run(
-        traces, mine, send, take.reshape(capacity, owners * slots), shards, share, scale, tables
-    )
-    return result.reshape(share, sources, LAGS)
+    return run(
+        traces, owner_lists, source_owner, source_slot, shards, owners, windows, scale, tables
+    )
 
 
 def solution(mesh):

time: 70.3 us -> 62.4 us (0.89)
  other arithmetic: 5.01 us -> 0 us
  matrix products: 1.47 us -> 0 us
  local copies, waits for them, and re-layouts: 7.07 us -> 5.96 us
    dot_general x1 -> x0, matrix products: 1.47 us -> none  [body(): mine = jnp.dot(pick, traces, preferred_element_type=f32).astype(bf16)]
    concatenate x2 -> x0, other arithmetic: 1.41 us -> none  [body(): ids = owner_lists[source_owner[:, None], source_slot].reshape(-1)]
    convert_element_type x3 -> x0, other arithmetic: 1.4 us -> none  [the longest x1 0.7 us: body(): rank = jnp.cumsum(matched.astype(jnp.int32), axis=1) - 1]
    gather x1 -> x0, local copies, waits for them, and re-layouts: 1.36 us -> none  [body(): ids = owner_lists[source_owner[:, None], source_slot].reshape(-1)]
    transpose x1, local copies, waits for them, and re-layouts: 2.74 us -> 4.09 us  [body(): jnp.transpose(raw_traces, (1, 0, 2)).reshape(windows * block, length)]
    convert_element_type x1 -> x0, local copies, waits for them, and re-layouts: 0.71 us -> none  [body(): take = (live[:, None, None] & (my_block[:, None, None] == jnp.arange(owne...]
    unnamed x3 -> x1, local copies, waits for them, and re-layouts: 2 us -> 1.87 us
where the time goes in v4:
time: 62.4 us; the launch traced here: 62.2 us
  Pallas kernels  56.2 us (90%)
  local copies, waits for them, and re-layouts  5.96 us (10%)
    pallas_call x1, Pallas kernels, run(): pl.pallas_call(functools.partial(kernel, owners, shards, block, windows,...  56.2 us
    transpose x1, local copies, waits for them, and re-layouts, body(): jnp.transpose(raw_traces, (1, 0, 2)).reshape(windows * block, length)  4.09 us
    unnamed x1, local copies, waits for them, and re-layouts  1.87 us

profile of v4, /device:TPU:0, one launch (start us, length us, event | category | flops | bytes accessed | tf_op | source)
XLA Modules:
  0.0 62.2 jit_solution(17610267308637165394)
XLA Ops:
  0.0 4.1 %copy.11 = bf16[4,64,4096]{2,1,0:T(8,128)(2,1)} copy(bf16[4,64,4096]{2,0,1:T(4,128)(2,1)} %bitcast.3) | data formatting | bytes 4194304 | tf_op jit(solution)/shard_map/transpose | solution.py:486
  4.1 56.2 %correlations.1 = f32[32,16,256]{2,1,0:T(8,128)} custom-call(bf16[256,4096]{1,0:T(8,128)(2,1)} %bitcast.2, s32[8,128]{1,0:T(8,128)} %lists_s.1, s32[8,128]{1,0:T(8,128)} %lists_s.1, s32[2]{0:T(128)} %owner_s.1, s32[2,8]{1,0:T(2,128)} %slot_s.1, f32[1,4096]{1,0:T(1,128)} %constant.12.clone.taper_ref, f32[9,256]{1,0:T(8,128)} %constant.13.clone.cos_ref, ...), custom_call_target="tpu_custom_call" | custom-call | tf_op jit(solution)/shard_map/correlations/pallas_call | solution.py:447
  60.3 1.9 %copy.13 = f32[32,16,256]{2,1,0:T(8,128)} copy(f32[32,16,256]{2,1,0:T(8,128)} %correlations.1) | data formatting | bytes 1048576

commit v5 on v4

--- a/solution.py
+++ b/solution.py
@@ -473,7 +473,7 @@
         ]
         + sems(chunks, owners) + sems(chunks, owners)
         + sems(shards) + sems(PIECES, owners) + sems(PIECES, shards),
-        compiler_params=pltpu.CompilerParams(collective_id=0, has_side_effects=True),
+        compiler_params=pltpu.CompilerParams(collective_id=0, has_side_effects=True, vmem_limit_bytes=32 << 20),
         name="correlations",
     )(traces, lists, lists, source_owner, source_slot, *tables)
 

time: 62.4 us -> 58.3 us (0.934)
  local copies, waits for them, and re-layouts: 5.96 us -> 3.73 us
  Pallas kernels: 56.2 us -> 54.3 us
    pallas_call x1, Pallas kernels: 56.2 us -> 54.3 us  [run(): pl.pallas_call(functools.partial(kernel, owners, shards, block, windows,...]
    transpose x1, local copies, waits for them, and re-layouts: 4.09 us -> 2.89 us  [body(): jnp.transpose(raw_traces, (1, 0, 2)).reshape(windows * block, length)]
    unnamed x1 -> x19, local copies, waits for them, and re-layouts: 1.87 us -> 0.83 us
where the time goes in v5:
time: 58.3 us; the launch traced here: 58.1 us
  Pallas kernels  54.3 us (93%)
  local copies, waits for them, and re-layouts  3.73 us (6%)
    pallas_call x1, Pallas kernels, run(): pl.pallas_call(functools.partial(kernel, owners, shards, block, windows,...  54.3 us
    transpose x1, local copies, waits for them, and re-layouts, body(): jnp.transpose(raw_traces, (1, 0, 2)).reshape(windows * block, length)  2.89 us

profile of v5, /device:TPU:0, one launch (start us, length us, event | category | flops | bytes accessed | tf_op | source)
XLA Modules:
  0.0 58.1 jit_solution(5144725081602978457)
XLA Ops:
  0.0 0.0 copy-start
  0.0 0.0 copy-start.1
  0.0 0.0 copy-start.2
  0.0 0.0 copy-start.3
  0.0 0.0 copy-start.4
  0.0 0.0 copy-start.5
  0.0 0.0 copy-start.6
  0.0 0.0 copy-start.7
  0.0 0.0 copy-start.8
  0.1 2.9 %copy.11 = bf16[4,64,4096]{2,1,0:T(8,128)(2,1)S(1)} copy(bf16[4,64,4096]{2,0,1:T(4,128)(2,1)} %bitcast.3) | data formatting | bytes 4194304 | tf_op jit(solution)/shard_map/transpose | solution.py:486
  3.0 0.0 copy-done
  3.0 0.0 copy-done.1
  3.0 0.0 copy-done.2
  3.0 0.0 copy-done.3
  3.0 0.0 copy-done.4
  3.0 0.0 copy-done.5
  3.0 0.0 copy-done.6
  3.0 0.0 copy-done.7
  3.0 0.0 copy-done.8
  3.0 54.3 %correlations.1 = f32[32,16,256]{2,1,0:T(8,128)S(1)} custom-call(bf16[256,4096]{1,0:T(8,128)(2,1)S(1)} %bitcast.2, s32[8,128]{1,0:T(8,128)S(1)} %copy-done.5, s32[8,128]{1,0:T(8,128)S(1)} %copy-done.5, s32[2]{0:T(128)S(1)} %copy-done.8, s32[2,8]{1,0:T(2,128)S(1)} %copy-done.7, f32[1,4096]{1,0:T(1,128)S(1)} %copy-done.4, f32[9,256]{1,0:T(8,128)S(1)} %copy-done.3, ...), custom_call_target="tpu_custom_call" | custom-call | tf_op jit(solution)/shard_map/correlations/pallas_call | solution.py:447
  57.3 0.8 %copy.13 = f32[32,16,256]{2,1,0:T(8,128)} copy(f32[32,16,256]{2,1,0:T(8,128)S(1)} %correlations.1) | data formatting | bytes 1048576
Async XLA Ops:
  0.0 3.0 %copy-start = (bf16[4096,256]{1,0:T(8,128)(2,1)S(1)}, bf16[4096,256]{1,0:T(8,128)(2,1)}, u32[]{:S(2)}) copy-start(bf16[4096,256]{1,0:T(8,128)(2,1)} %constant.17.clone.inv_hbm) | copy-start | bytes 6291460
  0.0 3.0 %copy-start.1 = (bf16[512,512]{1,0:T(8,128)(2,1)S(1)}, bf16[512,512]{1,0:T(8,128)(2,1)}, u32[]{:S(2)}) copy-start(bf16[512,512]{1,0:T(8,128)(2,1)} %constant.15.clone.second_ref) | copy-start | bytes 1572868
  0.0 3.0 %copy-start.2 = (f32[9,256]{1,0:T(8,128)S(1)}, f32[9,256]{1,0:T(8,128)}, u32[]{:S(2)}) copy-start(f32[9,256]{1,0:T(8,128)} %constant.14.clone.sin_ref) | copy-start | bytes 27652
  0.0 3.0 %copy-start.3 = (f32[9,256]{1,0:T(8,128)S(1)}, f32[9,256]{1,0:T(8,128)}, u32[]{:S(2)}) copy-start(f32[9,256]{1,0:T(8,128)} %constant.13.clone.cos_ref) | copy-start | bytes 27652
  0.0 3.0 %copy-start.4 = (f32[1,4096]{1,0:T(1,128)S(1)}, f32[1,4096]{1,0:T(1,128)}, u32[]{:S(2)}) copy-start(f32[1,4096]{1,0:T(1,128)} %constant.12.clone.taper_ref) | copy-start | bytes 49156
  0.0 3.0 %copy-start.5 = (s32[8,128]{1,0:T(8,128)S(1)}, s32[8,128]{1,0:T(8,128)}, u32[]{:S(2)}) copy-start(s32[8,128]{1,0:T(8,128)} %lists_s.1) | copy-start | bytes 12292
  0.0 3.0 %copy-start.6 = (f32[16,128]{1,0:T(8,128)S(1)}, f32[16,128]{1,0:T(8,128)}, u32[]{:S(2)}) copy-start(f32[16,128]{1,0:T(8,128)} %constant.16.clone.count_ref) | copy-start | bytes 24580
  0.0 3.0 %copy-start.7 = (s32[2,8]{1,0:T(2,128)S(1)}, s32[2,8]{1,0:T(2,128)}, u32[]{:S(2)}) copy-start(s32[2,8]{1,0:T(2,128)} %slot_s.1) | copy-start | bytes 196
  0.0 3.0 %copy-start.8 = (s32[2]{0:T(128)S(1)}, s32[2]{0:T(128)}, u32[]{:S(2)}) copy-start(s32[2]{0:T(128)} %owner_s.1) | copy-start | bytes 28
